TPU v7x, 32 devices: a whole 2x2x4 slice. The times are simulated.
32 devices in a mesh: member: 2 (over x), grid: 16 (over z, y, core).
Axes of the slice: x: 2, y: 2, z: 4, core: 2. Of those that a mesh axis runs over, the one named last changes fastest.
Arguments:
- spectrum: bfloat16 [1152, 64, 256], P('grid', 'member'), parts along dimension 1, may hold values from -6 to 6
- ocean_currents: float32 [2, 75, 64, 256], P(None, None, ('member', 'grid')), parts along dimension 2, may hold values from -5 to 5
- wind_stress: float32 [2, 64, 256], P(None, ('member', 'grid')), parts along dimension 1, may hold values from -6 to 6
- land_mask: int32 [32, 256], replicated, may hold values 0 or 1
- bin_drift: float32 [2, 1152], replicated, may hold values from -2 to 2
- coupling_in: bfloat16 [1152, 2048], replicated, may hold values from -0.1875 to 0.1875
- coupling_out: bfloat16 [2048, 1152], replicated, may hold values from -0.125 to 0.125
- stokes_weight: bfloat16 [150, 1152], replicated, may hold values from -0.1875 to 0.1875
- mixing_inverse: float32 [75, 75], replicated, may hold values from -1 to 2
Outputs:
- spectrum_out: bfloat16 [1152, 64, 256], P('grid', 'member'), parts along dimension 1
- currents_out: float32 [2, 75, 64, 256], P(None, None, ('member', 'grid')), parts along dimension 2
There are 2 independent parts, one for each index of `member`. A program takes and returns all parts, laid end to end along the dimension named above; an argument that names none is the same for every part. Nothing has to cross between parts.
All inputs are finite; a program needn't handle non-finite values.
Results may differ from a plain program's by a relative error of at most 0.0061.
Values may be sent and summed in bfloat16 or wider, within the bound.
No kernel may reach another device: no remote copies, remote signals or barrier semaphores. Data moves between devices by JAX's collectives and lax.ppermute only.
A program may use at most 64 MiB of HBM per device.

v0:
```python
import math

import jax
import jax.numpy as jnp
from jax import lax
from jax.sharding import PartitionSpec as P

STEPS = 2


time_step = 0.4
diffusion = 0.15
reach = 0.45


def padded_2(value, sides, width):
    for axis, dim in sides:
        size, length = (lax.axis_size(axis), value.shape[dim])
        up = [(i, (i + 1) % size) for i in range(size - 1)]
        down = [(j, i) for i, j in up]
        last = lax.slice_in_dim(value, length - width, length, axis=dim)
        first = lax.slice_in_dim(value, 0, width, axis=dim)
        before = lax.ppermute(last, axis, up)
        after = lax.ppermute(first, axis, down)
        value = jnp.concatenate([before, value, after], axis=dim)
    return value


def advect(center, above, below, east_flow, north_flow, drift, land):
    speed_x = reach * jnp.tanh(drift[0][:, None, None] + east_flow[None])
    speed_y = reach * jnp.tanh(drift[1][:, None, None] + north_flow[None])
    western = jnp.roll(center, 1, axis=2)
    eastern = jnp.roll(center, -1, axis=2)
    change = jnp.maximum(speed_x, 0.0) * (center - western) + jnp.minimum(speed_x, 0.0) * (
        eastern - center
    )
    change = (
        change
        + jnp.maximum(speed_y, 0.0) * (center - above)
        + jnp.minimum(speed_y, 0.0) * (below - center)
    )
    return (center - change) * land[None]


def interact(points, coupling_in, coupling_out, stokes_weight):
    bins, rows, cols = points.shape
    flat = points.reshape(bins, rows * cols)
    terms = lax.dot_general(
        flat, coupling_in, (((0,), (0,)), ((), ())), preferred_element_type=jnp.float32
    )
    active = (terms * jnp.tanh(terms)).astype(jnp.bfloat16)
    source = lax.dot_general(
        coupling_out, active, (((0,), (1,)), ((), ())), preferred_element_type=jnp.float32
    )
    updated = (flat.astype(jnp.float32) + source).astype(jnp.bfloat16)
    profile = jnp.dot(stokes_weight, updated, preferred_element_type=jnp.float32)
    return (updated.reshape(bins, rows, cols), profile.reshape(2, -1, rows, cols))


def ocean_update(padded, stokes, wind, inverse, land, latitude):
    center = padded[:, :, 1:-1]
    lateral = diffusion * (
        padded[:, :, :-2]
        + padded[:, :, 2:]
        + jnp.roll(center, 1, axis=3)
        + jnp.roll(center, -1, axis=3)
        - 4.0 * center
    )
    coriolis = latitude[None, :, None]
    eastward = center[0] + time_step * coriolis * (center[1] + stokes[1]) + lateral[0]
    northward = center[1] - time_step * coriolis * (center[0] + stokes[0]) + lateral[1]
    eastward = eastward.at[0].add(time_step * wind[0])
    northward = northward.at[0].add(time_step * wind[1])
    forced = jnp.stack([eastward, northward])
    mixed = jnp.einsum("kl,slrc->skrc", inverse, forced, precision=lax.Precision.HIGHEST)
    return mixed * land[None, None]


def per_device(
    spectrum,
    ocean_currents,
    wind_stress,
    land_mask,
    bin_drift,
    coupling_in,
    coupling_out,
    stokes_weight,
    mixing_inverse,
):
    device = lax.axis_index("grid")
    device_count = lax.axis_size("grid")
    rows_dev = ocean_currents.shape[2]
    total_rows = rows_dev * device_count
    land = land_mask.astype(jnp.float32)
    land_local = lax.dynamic_slice_in_dim(land, device * rows_dev, rows_dev, 0)
    row_place = (device * rows_dev + jnp.arange(rows_dev, dtype=jnp.int32)).astype(jnp.float32)
    latitude = jnp.sin(math.pi * ((row_place + 0.5) / total_rows - 0.5))
    ocean = ocean_currents
    points = lax.all_to_all(spectrum, "grid", split_axis=1, concat_axis=0, tiled=True)
    for turn_index in range(STEPS):
        padded = padded_2(points, (("grid", 1),), 1).astype(jnp.float32)
        moved = advect(
            padded[:, 1:-1],
            padded[:, :-2],
            padded[:, 2:],
            ocean[0, 0],
            ocean[1, 0],
            bin_drift,
            land_local,
        ).astype(jnp.bfloat16)
        updated, stokes = interact(moved, coupling_in, coupling_out, stokes_weight)
        ocean_padded = padded_2(ocean, (("grid", 2),), 1)
        points = updated
        ocean = ocean_update(
            ocean_padded, stokes, wind_stress, mixing_inverse, land_local, latitude
        )
    spectra = lax.all_to_all(points, "grid", split_axis=0, concat_axis=1, tiled=True)
    return (spectra, ocean)


def solution(mesh):
    return jax.shard_map(
        per_device,
        mesh=mesh,
        in_specs=(
            P("grid", "member", None),
            P(None, None, ("member", "grid"), None),
            P(None, ("member", "grid"), None),
            P(),
            P(),
            P(),
            P(),
            P(),
            P(),
        ),
        out_specs=(P("grid", "member", None), P(None, None, ("member", "grid"), None)),
        check_vma=False,
    )
```

profile of v0, /device:TPU:13, one launch (start us, length us, event | category | flops | bytes accessed | tf_op | source)
XLA Modules:
  0.0 153.6 jit_solution(14504660099868624787)
XLA Ops:
  0.7 3.0 %copy.97 = bf16[72,32,256]{2,0,1:T(8,128)(2,1)} copy(bf16[72,32,256]{2,1,0:T(8,128)(2,1)} %param.17) | data formatting | bytes 2359296 | tf_op args[0]
  3.7 6.5 %all-to-all-start = ((bf16[72,32,256]{2,0,1:T(8,128)(2,1)}), bf16[72,32,256]{2,0,1:T(8,128)(2,1)S(1)}, u32[]{:S(2)}, u32[]{:S(2)}) async-start(bf16[72,32,256]{2,0,1:T(8,128)(2,1)} %copy.97), calls=%async_computation | async-start | bytes 2359296 | tf_op jit(solution)/shard_map/all_to_all | solution.py:99
  10.2 0.7 fusion.90
  11.0 3.4 %collective-permute-start.4 = (f32[2,75,1,256]{3,1,2,0:T(8,128)}, f32[2,75,1,256]{3,1,2,0:T(8,128)}, u32[]{:S(2)}, u32[]{:S(2)}) collective-permute-start(f32[2,75,1,256]{3,1,2,0:T(8,128)} %get-tuple-element.104), channel_id=1, source_target_pairs={{0,1},{1,2},{2,3},{3,4},{4,5},{5,6},{6,7},{7,8},{8,9},{9,10},{10,1... | collective-permute-start | bytes 460808 | tf_op jit(solution)/shard_map/ppermute | solution.py:23
  14.3 1.9 %collective-permute-start.5 = (f32[2,75,1,256]{3,1,2,0:T(8,128)}, f32[2,75,1,256]{3,1,2,0:T(8,128)}, u32[]{:S(2)}, u32[]{:S(2)}) collective-permute-start(f32[2,75,1,256]{3,1,2,0:T(8,128)} %get-tuple-element.105), channel_id=1, source_target_pairs={{1,0},{2,1},{3,2},{4,3},{5,4},{6,5},{7,6},{8,7},{9,8},{10,9},{11,1... | collective-permute-start | bytes 460808 | tf_op jit(solution)/shard_map/ppermute | solution.py:24
  16.3 0.6 slice_bitcast_fusion.9
  16.8 0.8 fusion.89
  17.6 0.8 fusion.88
  18.5 19.5 %all-to-all-done = bf16[72,32,256]{2,0,1:T(8,128)(2,1)S(1)} async-done(((bf16[72,32,256]{2,0,1:T(8,128)(2,1)}), bf16[72,32,256]{2,0,1:T(8,128)(2,1)S(1)}, u32[]{:S(2)}, u32[]{:S(2)}) %all-to-all-start) | async-done | bytes 1179680 | tf_op jit(solution)/shard_map/all_to_all | solution.py:99
  38.1 1.1 fusion.83
  39.1 4.1 %collective-permute-start = (bf16[1152,1,256]{2,0,1:T(8,128)(2,1)}, bf16[1152,1,256]{2,0,1:T(8,128)(2,1)S(1)}, u32[]{:S(2)}, u32[]{:S(2)}) collective-permute-start(bf16[1152,1,256]{2,0,1:T(8,128)(2,1)} %get-tuple-element.70), channel_id=1, source_target_pairs={{0,1},{1,2},{2,3},{3,4},{4,5},{5,6},{6,7},{7,8},{8,9},{9,10},{10,1... | collective-permute-start | bytes 1769480 | tf_op jit(solution)/shard_map/ppermute | solution.py:23
  43.3 1.9 %collective-permute-start.1 = (bf16[1152,1,256]{2,0,1:T(8,128)(2,1)}, bf16[1152,1,256]{2,0,1:T(8,128)(2,1)}, u32[]{:S(2)}, u32[]{:S(2)}) collective-permute-start(bf16[1152,1,256]{2,0,1:T(8,128)(2,1)} %get-tuple-element.71), channel_id=1, source_target_pairs={{1,0},{2,1},{3,2},{4,3},{5,4},{6,5},{7,6},{8,7},{9,8},{10,9},{11,1... | collective-permute-start | bytes 1769480 | tf_op jit(solution)/shard_map/ppermute | solution.py:24
  45.2 0.6 fusion.93
  45.8 0.7 dynamic-slice_convert_fusion
  46.5 0.6 sine_multiply_fusion
  47.2 2.0 %fusion.39 = f32[2,75,2,256]{3,1,2,0:T(8,128)} fusion(f32[2,75,1,256]{3,1,2,0:T(8,128)} %collective-permute-done.5, f32[2,75,2,256]{3,1,2,0:T(8,128)S(1)} %copy.103, f32[2,75,1,256]{3,1,2,0:T(8,128)} %collective-permute-done.4, f32[2,75,2,255]{3,1,2,0:T(8,128)S(1)} %copy-done.1, f32[2,75,2,1]{3,1,2,0:T(8,128)S(1)} %copy-done.3, ...), kind=kLoop, calls=%fused_computation.58 | loop fusion | flops 768000 | bytes 1536000 | tf_op jit(solution)/shard_map/mul | solution.py:62
  49.1 1.3 collective-permute-done
  50.4 5.4 %collective-permute-done.1 = bf16[1152,1,256]{2,0,1:T(8,128)(2,1)} collective-permute-done((bf16[1152,1,256]{2,0,1:T(8,128)(2,1)}, bf16[1152,1,256]{2,0,1:T(8,128)(2,1)}, u32[]{:S(2)}, u32[]{:S(2)}) %collective-permute-start.1) | collective-permute-done | bytes 589856 | tf_op jit(solution)/shard_map/ppermute | solution.py:24
  55.8 1.4 maximum_convert_fusion
  57.2 0.4 fusion.81
  57.6 0.8 fusion.80
  58.4 2.9 %fusion.17 = bf16[1152,2,256]{2,0,1:T(8,128)(2,1)S(1)} fusion(f32[1152,4,256]{2,0,1:T(8,128)S(1)} %maximum_convert_fusion, f32[1152,2,255]{2,0,1:T(8,128)S(1)} %get-tuple-element.65, f32[1152,2,1]{2,0,1:T(8,128)S(1)} %get-tuple-element.67, f32[1152,2,1]{2,0,1:T(8,128)S(1)} %get-tuple-element.66, f32[1152,2,255]{2,0,1:T(8,128)S(1)} %get-tuple-element.64, ...), kind=kLoop, calls=%fused_computation.24 | loop fusion | flops 14155776 | bytes 12991488 | tf_op jit(solution)/shard_map/convert_element_type | solution.py:110
  61.3 1.4 copy.99
  62.7 10.0 %fusion.4 = bf16[1152,512]{0,1:T(8,128)(2,1)S(1)} fusion(bf16[2048,1152]{1,0:T(8,128)(2,1)} %param.23, bf16[1152,512]{0,1:T(8,128)(2,1)} %bitcast.92, bf16[1152,2048]{1,0:T(8,128)(2,1)} %param.22), kind=kOutput, calls=%fused_computation.8 | convolution fusion | flops 4835704832 | bytes 11796480 | tf_op jit(solution)/shard_map/dot_general | solution.py:52
  72.7 0.6 convolution_bitcast_fusion.3
  73.6 0.8 squeeze.57
  74.4 0.6 copy.100
  75.1 1.1 fusion.82
  76.2 1.9 %collective-permute-start.2 = (bf16[1152,1,256]{2,0,1:T(8,128)(2,1)}, bf16[1152,1,256]{2,0,1:T(8,128)(2,1)S(1)}, u32[]{:S(2)}, u32[]{:S(2)}) collective-permute-start(bf16[1152,1,256]{2,0,1:T(8,128)(2,1)} %get-tuple-element.68), channel_id=1, source_target_pairs={{0,1},{1,2},{2,3},{3,4},{4,5},{5,6},{6,7},{7,8},{8,9},{9,10},{10,1... | collective-permute-start | bytes 1769480 | tf_op jit(solution)/shard_map/ppermute | solution.py:23
  78.1 3.1 %collective-permute-start.3 = (bf16[1152,1,256]{2,0,1:T(8,128)(2,1)}, bf16[1152,1,256]{2,0,1:T(8,128)(2,1)}, u32[]{:S(2)}, u32[]{:S(2)}) collective-permute-start(bf16[1152,1,256]{2,0,1:T(8,128)(2,1)} %get-tuple-element.69), channel_id=1, source_target_pairs={{1,0},{2,1},{3,2},{4,3},{5,4},{6,5},{7,6},{8,7},{9,8},{10,9},{11,1... | collective-permute-start | bytes 1769480 | tf_op jit(solution)/shard_map/ppermute | solution.py:24
  81.8 0.4 fusion.29
  82.3 2.9 %collective-permute-done.2 = bf16[1152,1,256]{2,0,1:T(8,128)(2,1)S(1)} collective-permute-done((bf16[1152,1,256]{2,0,1:T(8,128)(2,1)}, bf16[1152,1,256]{2,0,1:T(8,128)(2,1)S(1)}, u32[]{:S(2)}, u32[]{:S(2)}) %collective-permute-start.2) | collective-permute-done | bytes 589856 | tf_op jit(solution)/shard_map/ppermute | solution.py:23
  85.2 6.9 %collective-permute-done.3 = bf16[1152,1,256]{2,0,1:T(8,128)(2,1)} collective-permute-done((bf16[1152,1,256]{2,0,1:T(8,128)(2,1)}, bf16[1152,1,256]{2,0,1:T(8,128)(2,1)}, u32[]{:S(2)}, u32[]{:S(2)}) %collective-permute-start.3) | collective-permute-done | bytes 589856 | tf_op jit(solution)/shard_map/ppermute | solution.py:24
  92.1 1.4 maximum_convert_fusion.1
  93.9 0.8 fusion.78
  94.7 2.9 %fusion.10 = bf16[1152,2,256]{2,0,1:T(8,128)(2,1)S(1)} fusion(f32[1152,4,256]{2,0,1:T(8,128)S(1)} %maximum_convert_fusion.1, f32[1152,2,255]{2,0,1:T(8,128)S(1)} %get-tuple-element.61, f32[1152,2,1]{2,0,1:T(8,128)S(1)} %get-tuple-element.63, f32[1152,2,1]{2,0,1:T(8,128)S(1)} %get-tuple-element.62, f32[1152,2,255]{2,0,1:T(8,128)S(1)} %get-tuple-element.60, ...), kind=kLoop, calls=%fused_computation.15 | loop fusion | flops 14155776 | bytes 12991488 | tf_op jit(solution)/shard_map/convert_element_type | solution.py:110
  97.5 1.4 copy.121
  99.0 10.0 %fusion.5 = bf16[1152,512]{0,1:T(8,128)(2,1)S(1)} fusion(bf16[2048,1152]{1,0:T(8,128)(2,1)} %param.23, bf16[1152,512]{0,1:T(8,128)(2,1)} %bitcast.93, bf16[1152,2048]{1,0:T(8,128)(2,1)} %param.22), kind=kOutput, calls=%fused_computation.9 | convolution fusion | flops 4835704832 | bytes 11796480 | tf_op jit(solution)/shard_map/dot_general | solution.py:52
  108.9 2.7 %copy.122 = bf16[1152,2,256]{2,1,0:T(2,128)(2,1)} copy(bf16[1152,2,256]{0,2,1:T(8,128)(2,1)S(1)} %bitcast.87) | data formatting | bytes 2359296 | tf_op jit(solution)/shard_map/reshape | solution.py:57
  111.6 7.9 %all-to-all-start.1 = ((bf16[1152,2,256]{2,1,0:T(2,128)(2,1)}), bf16[1152,2,256]{2,1,0:T(2,128)(2,1)S(1)}, u32[]{:S(2)}, u32[]{:S(2)}) async-start(bf16[1152,2,256]{2,1,0:T(2,128)(2,1)} %copy.122), calls=%async_computation.1 | async-start | bytes 2359296 | tf_op jit(solution)/shard_map/all_to_all | solution.py:117
  119.6 3.4 %collective-permute-start.6 = (f32[2,75,1,256]{3,1,2,0:T(8,128)S(1)}, f32[2,75,1,256]{3,1,2,0:T(8,128)S(1)}, u32[]{:S(2)}, u32[]{:S(2)}) collective-permute-start(f32[2,75,1,256]{3,1,2,0:T(8,128)S(1)} %get-tuple-element.90), channel_id=1, source_target_pairs={{0,1},{1,2},{2,3},{3,4},{4,5},{5,6},{6,7},{7,8},{8,9},{9,10},{10,1... | collective-permute-start | bytes 460808 | tf_op jit(solution)/shard_map/ppermute | solution.py:23
  122.9 1.9 %collective-permute-start.7 = (f32[2,75,1,256]{3,1,2,0:T(8,128)S(1)}, f32[2,75,1,256]{3,1,2,0:T(8,128)S(1)}, u32[]{:S(2)}, u32[]{:S(2)}) collective-permute-start(f32[2,75,1,256]{3,1,2,0:T(8,128)S(1)} %get-tuple-element.91), channel_id=1, source_target_pairs={{1,0},{2,1},{3,2},{4,3},{5,4},{6,5},{7,6},{8,7},{9,8},{10,9},{11,1... | collective-permute-start | bytes 460808 | tf_op jit(solution)/shard_map/ppermute | solution.py:24
  125.1 22.2 %collective-permute-done.6 = f32[2,75,1,256]{3,1,2,0:T(8,128)S(1)} collective-permute-done((f32[2,75,1,256]{3,1,2,0:T(8,128)S(1)}, f32[2,75,1,256]{3,1,2,0:T(8,128)S(1)}, u32[]{:S(2)}, u32[]{:S(2)}) %collective-permute-start.6) | collective-permute-done | bytes 153632 | tf_op jit(solution)/shard_map/ppermute | solution.py:23
  147.3 1.7 %collective-permute-done.7 = f32[2,75,1,256]{3,1,2,0:T(8,128)S(1)} collective-permute-done((f32[2,75,1,256]{3,1,2,0:T(8,128)S(1)}, f32[2,75,1,256]{3,1,2,0:T(8,128)S(1)}, u32[]{:S(2)}, u32[]{:S(2)}) %collective-permute-start.7) | collective-permute-done | bytes 153632 | tf_op jit(solution)/shard_map/ppermute | solution.py:24
  149.2 0.6 convolution_bitcast_fusion.2
  150.7 0.4 fusion.28
  151.1 1.0 copy.131
  152.3 1.3 copy.130
  (70 shorter events, 3.0 us)
Async XLA Ops:
  0.6 72.0 %copy-start = (bf16[150,1152]{1,0:T(8,128)(2,1)S(1)}, bf16[150,1152]{1,0:T(8,128)(2,1)}, u32[]{:S(2)}) copy-start(bf16[150,1152]{1,0:T(8,128)(2,1)} %param.24) | copy-start | bytes 1036804
  0.6 9.5 %copy-start.5 = (f32[2,75,2,256]{3,2,1,0:T(2,128)S(1)}, f32[2,75,2,256]{3,2,1,0:T(2,128)}, u32[]{:S(2)}) copy-start(f32[2,75,2,256]{3,2,1,0:T(2,128)} %param.18) | copy-start | bytes 921604
  3.7 34.3 %all-to-all-start = ((bf16[72,32,256]{2,0,1:T(8,128)(2,1)}), bf16[72,32,256]{2,0,1:T(8,128)(2,1)S(1)}, u32[]{:S(2)}, u32[]{:S(2)}) async-start(bf16[72,32,256]{2,0,1:T(8,128)(2,1)} %copy.97), calls=%async_computation | async-start | bytes 2359296 | tf_op jit(solution)/shard_map/all_to_all | solution.py:99
  11.0 36.2 %collective-permute-start.4 = (f32[2,75,1,256]{3,1,2,0:T(8,128)}, f32[2,75,1,256]{3,1,2,0:T(8,128)}, u32[]{:S(2)}, u32[]{:S(2)}) collective-permute-start(f32[2,75,1,256]{3,1,2,0:T(8,128)} %get-tuple-element.104), channel_id=1, source_target_pairs={{0,1},{1,2},{2,3},{3,4},{4,5},{5,6},{6,7},{7,8},{8,9},{9,10},{10,1... | collective-permute-start | bytes 460808 | tf_op jit(solution)/shard_map/ppermute | solution.py:23
  14.3 32.8 %collective-permute-start.5 = (f32[2,75,1,256]{3,1,2,0:T(8,128)}, f32[2,75,1,256]{3,1,2,0:T(8,128)}, u32[]{:S(2)}, u32[]{:S(2)}) collective-permute-start(f32[2,75,1,256]{3,1,2,0:T(8,128)} %get-tuple-element.105), channel_id=1, source_target_pairs={{1,0},{2,1},{3,2},{4,3},{5,4},{6,5},{7,6},{8,7},{9,8},{10,9},{11,1... | collective-permute-start | bytes 460808 | tf_op jit(solution)/shard_map/ppermute | solution.py:24
  37.9 7.3 %copy-start.15 = (f32[2,2,256]{2,1,0:T(2,128)S(1)}, f32[2,2,256]{2,1,0:T(2,128)}, u32[]{:S(2)}) copy-start(f32[2,2,256]{2,1,0:T(2,128)} %param.19) | copy-start | bytes 12292
  38.0 9.1 %copy-start.11 = (f32[2,1152]{1,0:T(2,128)S(1)}, f32[2,1152]{1,0:T(2,128)}, u32[]{:S(2)}) copy-start(f32[2,1152]{1,0:T(2,128)} %param.21) | copy-start | bytes 27652
  38.0 9.1 %copy-start.1 = (f32[2,75,2,255]{3,1,2,0:T(8,128)S(1)}, f32[2,75,2,255]{3,1,2,0:T(8,128)}, u32[]{:S(2)}) copy-start(f32[2,75,2,255]{3,1,2,0:T(8,128)} %get-tuple-element.101) | copy-start | bytes 918004
  38.0 9.1 %copy-start.3 = (f32[2,75,2,1]{3,1,2,0:T(8,128)S(1)}, f32[2,75,2,1]{3,1,2,0:T(8,128)}, u32[]{:S(2)}) copy-start(f32[2,75,2,1]{3,1,2,0:T(8,128)} %get-tuple-element.103) | copy-start | bytes 3604
  39.1 11.3 %collective-permute-start = (bf16[1152,1,256]{2,0,1:T(8,128)(2,1)}, bf16[1152,1,256]{2,0,1:T(8,128)(2,1)S(1)}, u32[]{:S(2)}, u32[]{:S(2)}) collective-permute-start(bf16[1152,1,256]{2,0,1:T(8,128)(2,1)} %get-tuple-element.70), channel_id=1, source_target_pairs={{0,1},{1,2},{2,3},{3,4},{4,5},{5,6},{6,7},{7,8},{8,9},{9,10},{10,1... | collective-permute-start | bytes 1769480 | tf_op jit(solution)/shard_map/ppermute | solution.py:23
  43.3 12.5 %collective-permute-start.1 = (bf16[1152,1,256]{2,0,1:T(8,128)(2,1)}, bf16[1152,1,256]{2,0,1:T(8,128)(2,1)}, u32[]{:S(2)}, u32[]{:S(2)}) collective-permute-start(bf16[1152,1,256]{2,0,1:T(8,128)(2,1)} %get-tuple-element.71), channel_id=1, source_target_pairs={{1,0},{2,1},{3,2},{4,3},{5,4},{6,5},{7,6},{8,7},{9,8},{10,9},{11,1... | collective-permute-start | bytes 1769480 | tf_op jit(solution)/shard_map/ppermute | solution.py:24
  57.6 0.8 copy-start.13
  57.6 0.8 copy-start.14
  73.4 1.0 copy-start.8
  73.6 0.8 copy-start.9
  74.4 6.8 %copy-start.2 = (f32[2,75,2,256]{3,1,2,0:T(8,128)S(1)}, f32[2,75,2,256]{3,1,2,0:T(8,128)}, u32[]{:S(2)}) copy-start(f32[2,75,2,256]{3,1,2,0:T(8,128)} %fusion.39) | copy-start | bytes 921604
  74.4 6.8 %copy-start.12 = (f32[2]{0:T(128)S(1)}, f32[2]{0:T(128)}, u32[]{:S(2)}) copy-start(f32[2]{0:T(128)} %sine_multiply_fusion) | copy-start | bytes 28
  75.0 6.2 %copy-start.4 = (f32[1,75,2,256]{3,2,1,0:T(2,128)S(1)}, f32[1,75,2,256]{3,2,1,0:T(2,128)}, u32[]{:S(2)}) copy-start(f32[1,75,2,256]{3,2,1,0:T(2,128)} %squeeze.57) | copy-start | bytes 460804
  75.0 6.4 %slice-start = ((f32[75,2,256]{2,1,0:T(2,128)}), f32[1,2,256]{2,1,0:T(2,128)S(1)}, s32[]{:S(2)}) async-start(f32[75,2,256]{2,1,0:T(2,128)} %copy-done.8), calls=%async_computation.2 | async-start | bytes 4096 | tf_op jit(solution)/shard_map/slice.162
  75.0 6.4 %slice-start.1 = ((f32[75,2,256]{2,1,0:T(2,128)}), f32[1,2,256]{2,1,0:T(2,128)S(1)}, s32[]{:S(2)}) async-start(f32[75,2,256]{2,1,0:T(2,128)} %copy-done.9), calls=%async_computation.3 | async-start | bytes 4096 | tf_op jit(solution)/shard_map/slice.163
  75.1 6.4 %copy-start.10 = (f32[1,2,256]{2,1,0:T(2,128)S(1)}, f32[1,2,256]{2,1,0:T(2,128)}, u32[]{:S(2)}) copy-start(f32[1,2,256]{2,1,0:T(2,128)} %get-tuple-element.113) | copy-start | bytes 6148
  75.1 6.7 %copy-start.6 = (f32[75,75]{1,0:T(8,128)S(1)}, f32[75,75]{1,0:T(8,128)}, u32[]{:S(2)}) copy-start(f32[75,75]{1,0:T(8,128)} %param.25) | copy-start | bytes 67504
  76.2 9.0 %collective-permute-start.2 = (bf16[1152,1,256]{2,0,1:T(8,128)(2,1)}, bf16[1152,1,256]{2,0,1:T(8,128)(2,1)S(1)}, u32[]{:S(2)}, u32[]{:S(2)}) collective-permute-start(bf16[1152,1,256]{2,0,1:T(8,128)(2,1)} %get-tuple-element.68), channel_id=1, source_target_pairs={{0,1},{1,2},{2,3},{3,4},{4,5},{5,6},{6,7},{7,8},{8,9},{9,10},{10,1... | collective-permute-start | bytes 1769480 | tf_op jit(solution)/shard_map/ppermute | solution.py:23
  78.1 14.0 %collective-permute-start.3 = (bf16[1152,1,256]{2,0,1:T(8,128)(2,1)}, bf16[1152,1,256]{2,0,1:T(8,128)(2,1)}, u32[]{:S(2)}, u32[]{:S(2)}) collective-permute-start(bf16[1152,1,256]{2,0,1:T(8,128)(2,1)} %get-tuple-element.69), channel_id=1, source_target_pairs={{1,0},{2,1},{3,2},{4,3},{5,4},{6,5},{7,6},{8,7},{9,8},{10,9},{11,1... | collective-permute-start | bytes 1769480 | tf_op jit(solution)/shard_map/ppermute | solution.py:24
  111.6 40.5 %all-to-all-start.1 = ((bf16[1152,2,256]{2,1,0:T(2,128)(2,1)}), bf16[1152,2,256]{2,1,0:T(2,128)(2,1)S(1)}, u32[]{:S(2)}, u32[]{:S(2)}) async-start(bf16[1152,2,256]{2,1,0:T(2,128)(2,1)} %copy.122), calls=%async_computation.1 | async-start | bytes 2359296 | tf_op jit(solution)/shard_map/all_to_all | solution.py:117
  119.6 27.8 %collective-permute-start.6 = (f32[2,75,1,256]{3,1,2,0:T(8,128)S(1)}, f32[2,75,1,256]{3,1,2,0:T(8,128)S(1)}, u32[]{:S(2)}, u32[]{:S(2)}) collective-permute-start(f32[2,75,1,256]{3,1,2,0:T(8,128)S(1)} %get-tuple-element.90), channel_id=1, source_target_pairs={{0,1},{1,2},{2,3},{3,4},{4,5},{5,6},{6,7},{7,8},{8,9},{9,10},{10,1... | collective-permute-start | bytes 460808 | tf_op jit(solution)/shard_map/ppermute | solution.py:23
  122.9 26.1 %collective-permute-start.7 = (f32[2,75,1,256]{3,1,2,0:T(8,128)S(1)}, f32[2,75,1,256]{3,1,2,0:T(8,128)S(1)}, u32[]{:S(2)}, u32[]{:S(2)}) collective-permute-start(f32[2,75,1,256]{3,1,2,0:T(8,128)S(1)} %get-tuple-element.91), channel_id=1, source_target_pairs={{1,0},{2,1},{3,2},{4,3},{5,4},{6,5},{7,6},{8,7},{9,8},{10,9},{11,1... | collective-permute-start | bytes 460808 | tf_op jit(solution)/shard_map/ppermute | solution.py:24
  149.8 0.9 copy-start.7
where the time goes:
time: 154 us
  waiting for transfers between devices  59.8 us (39%)
  starting transfers between devices  36.1 us (23%)
  matrix products  22 us (14%)
  local copies, waits for them, and re-layouts  21.9 us (14%)
  other arithmetic  12.6 us (8%)
    ppermute x4, waiting for transfers between devices, padded_2(): before = lax.ppermute(last, axis, up)  26.4 us
    dot_general x2, matrix products, interact(): lax.dot_general(coupling_out, active, (((0,), (1,)), ((), ())), preferred...  19.9 us
    all_to_all x1, waiting for transfers between devices, per_device(): lax.all_to_all(spectrum, 'grid', split_axis=1, concat_axis=0, tiled=True)  19.5 us
    ppermute x4, waiting for transfers between devices, padded_2(): after = lax.ppermute(first, axis, down)  13.9 us
    ppermute x4, starting transfers between devices, padded_2(): before = lax.ppermute(last, axis, up)  12.8 us
    ppermute x4, starting transfers between devices, padded_2(): after = lax.ppermute(first, axis, down)  8.86 us
    all_to_all x1, starting transfers between devices, per_device(): lax.all_to_all(points, 'grid', split_axis=0, concat_axis=1, tiled=True)  7.94 us
    all_to_all x1, starting transfers between devices, per_device(): lax.all_to_all(spectrum, 'grid', split_axis=1, concat_axis=0, tiled=True)  6.52 us
  transfers between devices with their start and end apart: 10, of which 7 were waited for; matrix products, arithmetic and copies ran while one was open for 8% of the time, Pallas kernels for 0%

commit v1 on v0

--- a/solution.py
+++ b/solution.py
@@ -1,16 +1,306 @@
+import functools
 import math
 
 import jax
 import jax.numpy as jnp
 from jax import lax
+from jax.experimental import pallas as pl
+from jax.experimental.pallas import tpu as pltpu
 from jax.sharding import PartitionSpec as P
 
 STEPS = 2
-
 
 time_step = 0.4
 diffusion = 0.15
 reach = 0.45
+VMEM = pl.BlockSpec(memory_space=pltpu.VMEM)
+LIMIT = 60 * 1024 * 1024
+
+
+def upwind(f, above, below, drift_x, drift_y, east, north, land):
+    cols = f.shape[1]
+    speed_x = reach * jnp.tanh(drift_x + east)
+    speed_y = reach * jnp.tanh(drift_y + north)
+    west = f - pltpu.roll(f, 1, 1)
+    step_x = jnp.where(speed_x > 0.0, west, pltpu.roll(west, cols - 1, 1))
+    step_y = jnp.where(speed_y > 0.0, f - above, below - f)
+    return (f - (speed_x * step_x + speed_y * step_y)) * land
+
+
+def wide(ref, axis, rows, cols):
+    part = ref[axis, rows, :]
+    return jnp.concatenate([part] * (cols // part.shape[1]), axis=1)
+
+
+def move_bins_kernel(me_ref, spec_ref, ocean_ref, land_ref, drift_ref, out_ref, *planes):
+    bins, rows, cols = spec_ref.shape
+    devices, _, row_dev, _ = ocean_ref.shape
+    first = pl.multiple_of(me_ref[0] * bins, 8)
+
+    @pl.loop(0, bins)
+    def _(b):
+        plane = spec_ref[b].astype(jnp.float32)
+        for h, ref in enumerate(planes):
+            ref[pl.ds(b * rows, rows), :] = plane[:, h * 128 : (h + 1) * 128]
+
+    size = 24 if bins % 24 == 0 else 8
+
+    def row(b, r):
+        return jnp.concatenate(
+            [ref[pl.ds(b * rows + r, size, stride=rows), :] for ref in planes], axis=1
+        )
+
+    @pl.loop(0, devices)
+    def _(d):
+        for j in range(row_dev):
+            r = d * row_dev + j
+            land = land_ref[pl.ds(r, 1), :].astype(jnp.float32)
+            east, north = (ocean_ref[d, s, j : j + 1, :] for s in range(2))
+            for b in range(0, bins, size):
+                f = row(b, r)
+                above = row(b, jnp.maximum(r - 1, 0))
+                below = row(b, jnp.minimum(r + 1, rows - 1))
+                above = jnp.where(r > 0, above, 0.0)
+                below = jnp.where(r < rows - 1, below, 0.0)
+                here = pl.ds(pl.multiple_of(first + b, 8), size)
+                moved = upwind(
+                    f, above, below, wide(drift_ref, 0, here, cols), wide(drift_ref, 1, here, cols), east, north, land
+                )
+                out_ref[d, b : b + size, j * cols : (j + 1) * cols] = moved.astype(jnp.bfloat16)
+
+
+def move_bins(me, spectrum, ocean_top, land_mask, drift):
+    bins, rows, cols = spectrum.shape
+    devices, _, row_dev, _ = ocean_top.shape
+    return pl.pallas_call(
+        move_bins_kernel,
+        out_shape=jax.ShapeDtypeStruct((devices, bins, row_dev * cols), jnp.bfloat16),
+        in_specs=[pl.BlockSpec(memory_space=pltpu.SMEM)] + [VMEM] * 4,
+        out_specs=VMEM,
+        scratch_shapes=[pltpu.VMEM((bins * rows, 128), jnp.float32)] * (cols // 128),
+        compiler_params=pltpu.CompilerParams(vmem_limit_bytes=20 * 1024 * 1024),
+        cost_estimate=pl.CostEstimate(flops=40 * spectrum.size, bytes_accessed=4 * spectrum.size, transcendentals=2 * spectrum.size),
+        name="move_bins",
+    )(me, spectrum, ocean_top, land_mask, drift)
+
+
+def tile_of(total, most):
+    return next(t for t in range(most - most % 8, 0, -8) if total % t == 0)
+
+
+def interact_body(moved_ref, win_ref, wout_ref, stokes_ref, active, updated_refs, whole, profile_ref, tk, tm):
+    terms_count, bins = win_ref.shape
+
+    @pl.loop(0, terms_count // tk)
+    def _(i):
+        at = pl.ds(pl.multiple_of(i * tk, tk), tk)
+        terms = jnp.dot(win_ref[at, :], moved_ref[...], preferred_element_type=jnp.float32)
+        active[at, :] = (terms * jnp.tanh(terms)).astype(jnp.bfloat16)
+
+    @pl.loop(0, bins // tm)
+    def _(i):
+        at = pl.ds(pl.multiple_of(i * tm, 8), tm)
+        source = jnp.dot(wout_ref[at, :], active[...], preferred_element_type=jnp.float32)
+        updated = (moved_ref[at, :].astype(jnp.float32) + source).astype(jnp.bfloat16)
+        whole[at, :] = updated
+        width = updated.shape[1] // max(1, len(updated_refs))
+        for j, ref in enumerate(updated_refs):
+            ref[at, :] = updated[:, j * width : (j + 1) * width]
+
+    for s in range(2):
+        profile_ref[s] = jnp.dot(stokes_ref[s], whole[...], preferred_element_type=jnp.float32)
+
+
+def first_kernel(moved_ref, win_ref, wout_ref, stokes_ref, *refs):
+    *updated_refs, profile_ref, active, whole = refs
+    tk, tm = tile_of(win_ref.shape[0], 1024), tile_of(wout_ref.shape[0], 576)
+    interact_body(moved_ref, win_ref, wout_ref, stokes_ref, active, updated_refs, whole, profile_ref, tk, tm)
+
+
+def first_step(moved, win, wout, stokes, row_dev):
+    bins, points = moved.shape
+    terms, levels = win.shape[0], stokes.shape[1]
+    return pl.pallas_call(
+        first_kernel,
+        out_shape=[jax.ShapeDtypeStruct((bins, points // row_dev), jnp.bfloat16)] * row_dev
+        + [jax.ShapeDtypeStruct((2, levels, points), jnp.float32)],
+        in_specs=[VMEM] * 4,
+        out_specs=[VMEM] * (row_dev + 1),
+        scratch_shapes=[pltpu.VMEM((terms, points), jnp.bfloat16), pltpu.VMEM((bins, points), jnp.bfloat16)],
+        compiler_params=pltpu.CompilerParams(vmem_limit_bytes=24 * 1024 * 1024),
+        cost_estimate=pl.CostEstimate(flops=4 * bins * terms * points, bytes_accessed=4 * bins * terms, transcendentals=terms * points),
+        name="first_step",
+    )(moved, win, wout, stokes)
+
+
+def second_kernel(win_ref, wout_ref, stokes_ref, drift_ref, ocean_ref, land_ref, *refs):
+    *row_refs, whole, profile_ref, active, moved = refs
+    bins, cols = row_refs[0].shape
+    row_dev = len(row_refs) - 2
+    size = 16
+
+    @pl.loop(0, bins // size)
+    def _(i):
+        at = pl.ds(pl.multiple_of(i * size, size), size)
+        rows = [ref[at, :].astype(jnp.float32) for ref in row_refs]
+        drift_x, drift_y = (wide(drift_ref, s, at, cols) for s in range(2))
+        for j in range(row_dev):
+            lanes = slice(j * cols, (j + 1) * cols)
+            east, north = (ocean_ref[s, 0:1, lanes] for s in range(2))
+            new = upwind(rows[j + 1], rows[j], rows[j + 2], drift_x, drift_y, east, north, land_ref[:, lanes])
+            moved[at, lanes] = new.astype(jnp.bfloat16)
+
+    tk, tm = tile_of(win_ref.shape[0], 1024), tile_of(wout_ref.shape[0], 576)
+    interact_body(moved, win_ref, wout_ref, stokes_ref, active, (), whole, profile_ref, tk, tm)
+
+
+def second_step(rows, win, wout, stokes, drift, ocean, land):
+    bins, cols = rows[0].shape
+    points = cols * (len(rows) - 2)
+    terms, levels = win.shape[0], stokes.shape[1]
+    return pl.pallas_call(
+        second_kernel,
+        out_shape=[
+            jax.ShapeDtypeStruct((bins, points), jnp.bfloat16),
+            jax.ShapeDtypeStruct((2, levels, points), jnp.float32),
+        ],
+        in_specs=[VMEM] * (6 + len(rows)),
+        out_specs=[VMEM] * 2,
+        scratch_shapes=[pltpu.VMEM((terms, points), jnp.bfloat16), pltpu.VMEM((bins, points), jnp.bfloat16)],
+        compiler_params=pltpu.CompilerParams(vmem_limit_bytes=24 * 1024 * 1024),
+        cost_estimate=pl.CostEstimate(flops=4 * bins * terms * points, bytes_accessed=4 * bins * terms, transcendentals=terms * points),
+        name="second_step",
+    )(win, wout, stokes, drift, ocean, land, *rows)
+
+
+def ocean_kernel(ocean_ref, above_ref, below_ref, profile_ref, wind_ref, inverse_ref, land_ref, latitude_ref, out_ref):
+    levels, points = ocean_ref.shape[1:]
+    cols = above_ref.shape[2]
+    row_dev = points // cols
+    turn = time_step * latitude_ref[...]
+    top = lax.broadcasted_iota(jnp.int32, (levels, points), 0) == 0
+    for s in range(2):
+        center = ocean_ref[s]
+        other = ocean_ref[1 - s] + profile_ref[1 - s]
+        pieces = [center[:, j * cols : (j + 1) * cols] for j in range(row_dev)]
+        rows = [above_ref[s]] + pieces + [below_ref[s]]
+        around = [
+            rows[j] + rows[j + 2] + pltpu.roll(rows[j + 1], 1, 1) + pltpu.roll(rows[j + 1], cols - 1, 1)
+            for j in range(row_dev)
+        ]
+        lateral = diffusion * (jnp.concatenate(around, axis=1) - 4.0 * center)
+        swing = turn * other
+        forced = center + (swing if s == 0 else -swing) + lateral
+        forced = forced + jnp.where(top, time_step * wind_ref[s : s + 1, :], 0.0)
+        mixed = jnp.dot(inverse_ref[...], forced, precision=lax.Precision.HIGHEST, preferred_element_type=jnp.float32)
+        out_ref[s] = mixed * land_ref[...]
+
+
+def ocean_step(ocean, above, below, profile, wind, inverse, land, latitude):
+    return pl.pallas_call(
+        ocean_kernel,
+        out_shape=jax.ShapeDtypeStruct(ocean.shape, jnp.float32),
+        in_specs=[VMEM] * 8,
+        out_specs=VMEM,
+        compiler_params=pltpu.CompilerParams(vmem_limit_bytes=8 * 1024 * 1024),
+        cost_estimate=pl.CostEstimate(flops=12 * inverse.shape[0] * ocean.size, bytes_accessed=12 * ocean.size, transcendentals=0),
+        name="ocean_step",
+    )(ocean, above, below, profile, wind, inverse, land, latitude)
+
+
+def gather_kernel(parts_ref, out_ref, *planes):
+    devices, bins, points = parts_ref.shape
+    rows, cols = out_ref.shape[1:]
+    row_dev = rows // devices
+    size = 24 if bins % 24 == 0 else 8
+
+    @pl.loop(0, devices)
+    def _(d):
+        for b in range(0, bins, size):
+            part = parts_ref[d, b : b + size, :].astype(jnp.float32)
+            for j in range(row_dev):
+                at = pl.ds(b * rows + d * row_dev + j, size, stride=rows)
+                for h, ref in enumerate(planes):
+                    low = j * cols + h * 128
+                    ref[at, :] = part[:, low : low + 128]
+
+    @pl.loop(0, bins)
+    def _(b):
+        plane = [ref[pl.ds(b * rows, rows), :] for ref in planes]
+        out_ref[b] = jnp.concatenate(plane, axis=1).astype(jnp.bfloat16)
+
+
+def gather_rows(parts, rows, cols):
+    bins = parts.shape[1]
+    return pl.pallas_call(
+        gather_kernel,
+        out_shape=jax.ShapeDtypeStruct((bins, rows, cols), jnp.bfloat16),
+        in_specs=[VMEM],
+        out_specs=VMEM,
+        scratch_shapes=[pltpu.VMEM((bins * rows, 128), jnp.float32)] * (cols // 128),
+        compiler_params=pltpu.CompilerParams(vmem_limit_bytes=20 * 1024 * 1024),
+        cost_estimate=pl.CostEstimate(flops=parts.size, bytes_accessed=4 * parts.size, transcendentals=0),
+        name="gather_rows",
+    )(parts)
+
+
+def shifts(size):
+    up = [(i, i + 1) for i in range(size - 1)]
+    return up, [(j, i) for i, j in up]
+
+
+def exchange(value):
+    return lax.all_to_all(value, "grid", split_axis=0, concat_axis=0, tiled=True)
+
+
+def per_device(
+    spectrum,
+    ocean_currents,
+    wind_stress,
+    land_mask,
+    bin_drift,
+    coupling_in,
+    coupling_out,
+    stokes_weight,
+    mixing_inverse,
+):
+    device = lax.axis_index("grid")
+    devices = lax.axis_size("grid")
+    bins, rows, cols = spectrum.shape
+    row_dev = rows // devices
+    levels = ocean_currents.shape[1]
+    points = row_dev * cols
+    up, down = shifts(devices)
+    me = device.astype(jnp.int32).reshape(1)
+
+    tops = jnp.broadcast_to(ocean_currents[:, 0][None], (devices, 2, row_dev, cols))
+    tops = exchange(tops)
+    ocean_above = lax.ppermute(ocean_currents[:, :, -1], "grid", up)
+    ocean_below = lax.ppermute(ocean_currents[:, :, 0], "grid", down)
+
+    win = coupling_in.T
+    wout = coupling_out.T
+    stokes = stokes_weight.reshape(2, levels, -1)
+    drift = jnp.broadcast_to(bin_drift[:, :, None], bin_drift.shape + (128,))
+    land = lax.dynamic_slice_in_dim(land_mask, device * row_dev, row_dev, 0)
+    land = land.astype(jnp.float32).reshape(1, points)
+    place = (device * row_dev + jnp.arange(row_dev, dtype=jnp.int32)).astype(jnp.float32)
+    latitude = jnp.sin(math.pi * ((place + 0.5) / rows - 0.5))
+    latitude = jnp.broadcast_to(latitude[:, None], (row_dev, cols)).reshape(1, points)
+    wind = wind_stress.reshape(2, points)
+    ocean = ocean_currents.reshape(2, levels, points)
+
+    moved = exchange(move_bins(me, spectrum, tops, land_mask, drift))
+    *updated, profile = first_step(moved.reshape(-1, points), win, wout, stokes, row_dev)
+    above = lax.ppermute(updated[-1], "grid", up)
+    below = lax.ppermute(updated[0], "grid", down)
+    ocean = ocean_step(ocean, ocean_above, ocean_below, profile, wind, mixing_inverse, land, latitude)
+    whole, profile = second_step([above, *updated, below], win, wout, stokes, drift, ocean, land)
+    spectra = exchange(whole.reshape(devices, bins, points))
+    ocean_above = lax.ppermute(ocean[:, :, -cols:], "grid", up)
+    ocean_below = lax.ppermute(ocean[:, :, :cols], "grid", down)
+    ocean = ocean_step(ocean, ocean_above, ocean_below, profile, wind, mixing_inverse, land, latitude)
+    return gather_rows(spectra, rows, cols), ocean.reshape(2, levels, row_dev, cols)
 
 
 def padded_2(value, sides, width):
@@ -26,7 +316,7 @@
     return value
 
 
-def advect(center, above, below, east_flow, north_flow, drift, land):
+def plain_advect(center, above, below, east_flow, north_flow, drift, land):
     speed_x = reach * jnp.tanh(drift[0][:, None, None] + east_flow[None])
     speed_y = reach * jnp.tanh(drift[1][:, None, None] + north_flow[None])
     western = jnp.roll(center, 1, axis=2)
@@ -42,7 +332,7 @@
     return (center - change) * land[None]
 
 
-def interact(points, coupling_in, coupling_out, stokes_weight):
+def plain_interact(points, coupling_in, coupling_out, stokes_weight):
     bins, rows, cols = points.shape
     flat = points.reshape(bins, rows * cols)
     terms = lax.dot_general(
@@ -57,7 +347,7 @@
     return (updated.reshape(bins, rows, cols), profile.reshape(2, -1, rows, cols))
 
 
-def ocean_update(padded, stokes, wind, inverse, land, latitude):
+def plain_ocean_update(padded, stokes, wind, inverse, land, latitude):
     center = padded[:, :, 1:-1]
     lateral = diffusion * (
         padded[:, :, :-2]
@@ -76,7 +366,7 @@
     return mixed * land[None, None]
 
 
-def per_device(
+def plain_device(
     spectrum,
     ocean_currents,
     wind_stress,
@@ -99,7 +389,7 @@
     points = lax.all_to_all(spectrum, "grid", split_axis=1, concat_axis=0, tiled=True)
     for turn_index in range(STEPS):
         padded = padded_2(points, (("grid", 1),), 1).astype(jnp.float32)
-        moved = advect(
+        moved = plain_advect(
             padded[:, 1:-1],
             padded[:, :-2],
             padded[:, 2:],
@@ -108,10 +398,10 @@
             bin_drift,
             land_local,
         ).astype(jnp.bfloat16)
-        updated, stokes = interact(moved, coupling_in, coupling_out, stokes_weight)
+        updated, stokes = plain_interact(moved, coupling_in, coupling_out, stokes_weight)
         ocean_padded = padded_2(ocean, (("grid", 2),), 1)
         points = updated
-        ocean = ocean_update(
+        ocean = plain_ocean_update(
             ocean_padded, stokes, wind_stress, mixing_inverse, land_local, latitude
         )
     spectra = lax.all_to_all(points, "grid", split_axis=0, concat_axis=1, tiled=True)
@@ -119,8 +409,12 @@
 
 
 def solution(mesh):
+    def body(spectrum, *others):
+        aligned = spectrum.shape[0] % 8 == 0 and spectrum.shape[2] % 128 == 0
+        return (per_device if aligned else plain_device)(spectrum, *others)
+
     return jax.shard_map(
-        per_device,
+        body,
         mesh=mesh,
         in_specs=(
             P("grid", "member", None),

time: 154 us -> 156 us (1.013)
  Pallas kernels: 0 us -> 40.8 us
  matrix products: 22 us -> 0 us
  other arithmetic: 12.6 us -> 0.06 us
  waiting for transfers between devices: 59.8 us -> 47.7 us
  local copies, waits for them, and re-layouts: 21.9 us -> 27 us
  starting transfers between devices: 36.1 us -> 38.2 us
    pallas_call x0 -> x6, Pallas kernels: none -> 40.8 us  [the longest x1 19.8 us: second_step(): pl.pallas_call(second_kernel, out_shape=[jax.ShapeDtypeStruct((bins, poin...]
    dot_general x6 -> x0, matrix products: 22 us -> none  [the longest x2 19.9 us: interact(): lax.dot_general(coupling_out, active, (((0,), (1,)), ((), ())), preferred...]
    unnamed x37 -> x28, local copies, waits for them, and re-layouts: 5.35 us -> 23 us
    ppermute x8 -> x6, waiting for transfers between devices: 40.3 us -> 29.3 us  [the longest x1 22.5 us: per_device(): ocean_above = lax.ppermute(ocean[:, :, -cols:], 'grid', up)]
    convert_element_type x5 -> x0, other arithmetic: 9.3 us -> none  [the longest x2 5.73 us: per_device(): moved = advect(padded[:, 1:-1], padded[:, :-2], padded[:, 2:], ocean[0, 0...]
    slice x17 -> x2, local copies, waits for them, and re-layouts: 7.76 us -> 0.26 us  [the longest x1 0.24 us: per_device(): ocean_below = lax.ppermute(ocean_currents[:, :, 0], 'grid', down)]
    all_to_all x2 -> x3, starting transfers between devices: 14.5 us -> 20.8 us  [exchange(): lax.all_to_all(value, 'grid', split_axis=0, concat_axis=0, tiled=True)]
    ppermute x8 -> x6, starting transfers between devices: 21.6 us -> 17.3 us  [the longest x1 4.54 us: per_device(): ocean_above = lax.ppermute(ocean_currents[:, :, -1], 'grid', up)]
  transfers between devices with their start and end apart: 10 -> 9, of which waited for: 7 -> 5; matrix products, arithmetic and copies ran while one was open for 8% -> 10% of each run, Pallas kernels for 0% -> 1%
where the time goes in v1:
time: 156 us; the launch traced here: 155 us
  waiting for transfers between devices  47.7 us (31%)
  Pallas kernels  40.8 us (26%)
  starting transfers between devices  38.2 us (24%)
  local copies, waits for them, and re-layouts  27 us (17%)
    unnamed x28, local copies, waits for them, and re-layouts  23 us
    ppermute x1, waiting for transfers between devices, per_device(): ocean_above = lax.ppermute(ocean[:, :, -cols:], 'grid', up)  22.5 us
    all_to_all x3, starting transfers between devices, exchange(): lax.all_to_all(value, 'grid', split_axis=0, concat_axis=0, tiled=True)  20.8 us
    pallas_call x1, Pallas kernels, second_step(): pl.pallas_call(second_kernel, out_shape=[jax.ShapeDtypeStruct((bins, poin...  19.8 us
    all_to_all x3, waiting for transfers between devices, exchange(): lax.all_to_all(value, 'grid', split_axis=0, concat_axis=0, tiled=True)  18.4 us
    pallas_call x1, Pallas kernels, move_bins(): pl.pallas_call(move_bins_kernel, out_shape=jax.ShapeDtypeStruct((devices,...  9.27 us
    pallas_call x1, Pallas kernels, first_step(): pl.pallas_call(first_kernel, out_shape=[jax.ShapeDtypeStruct((bins, point...  6.87 us
    ppermute x1, waiting for transfers between devices, per_device(): ocean_below = lax.ppermute(ocean_currents[:, :, 0], 'grid', down)  5.17 us
  transfers between devices with their start and end apart: 9, of which 5 were waited for; matrix products, arithmetic and copies ran while one was open for 10% of the time, Pallas kernels for 1%

profile of v1, /device:TPU:13, one launch (start us, length us, event | category | flops | bytes accessed | tf_op | source)
XLA Modules:
  0.0 154.7 jit_solution(15481158012613698992)
XLA Ops:
  0.6 0.0 copy-start.6
  0.6 0.0 copy-start.4
  0.6 0.8 slice_bitcast_fusion
  1.4 0.6 broadcast_in_dim.10
  2.1 6.5 %all-to-all-start = ((f32[16,2,2,256]{3,2,1,0:T(2,128)}), f32[16,2,2,256]{3,2,1,0:T(2,128)S(1)}, u32[]{:S(2)}, u32[]{:S(2)}) async-start(f32[16,2,2,256]{3,2,1,0:T(2,128)} %broadcast_in_dim.10), calls=%async_computation | async-start | bytes 131072 | tf_op jit(solution)/shard_map/all_to_all | solution.py:253
  8.6 4.3 %all-to-all-done.ocean_ref = f32[16,2,2,256]{3,2,1,0:T(2,128)S(1)} async-done(((f32[16,2,2,256]{3,2,1,0:T(2,128)}), f32[16,2,2,256]{3,2,1,0:T(2,128)S(1)}, u32[]{:S(2)}, u32[]{:S(2)}) %all-to-all-start) | async-done | bytes 65568 | tf_op jit(solution)/shard_map/all_to_all | solution.py:253
  12.9 1.1 broadcast_in_dim.8.drift_ref
  14.0 0.0 copy-done.6
  14.0 0.0 copy-done.4
  14.0 9.3 %move_bins.1 = bf16[16,72,512]{2,1,0:T(8,128)(2,1)} custom-call(s32[1]{0:T(128)} %bitcast.4.me_ref, bf16[72,32,256]{2,1,0:T(8,128)(2,1)S(1)} %copy-done.4, f32[16,2,2,256]{3,2,1,0:T(2,128)S(1)} %all-to-all-done.ocean_ref, s32[32,256]{1,0:T(8,128)S(1)} %copy-done.6, f32[2,1152,128]{2,1,0:T(8,128)S(1)} %broadcast_in_dim.8.drift_ref), custom_call_target="tpu_custom_call" | custom-call | flops 23592960 | bytes 2359296 | tf_op jit(solution)/shard_map/move_bins/pallas_call | solution.py:75
  23.2 6.2 %all-to-all-start.1 = ((bf16[16,72,512]{2,1,0:T(8,128)(2,1)}), bf16[16,72,512]{2,1,0:T(8,128)(2,1)S(1)}, u32[]{:S(2)}, u32[]{:S(2)}) async-start(bf16[16,72,512]{2,1,0:T(8,128)(2,1)} %move_bins.1), calls=%async_computation.1 | async-start | bytes 2359296 | tf_op jit(solution)/shard_map/all_to_all | solution.py:253
  29.5 6.7 %copy.15 = bf16[1152,2048]{0,1:T(8,128)(2,1)} copy(bf16[1152,2048]{1,0:T(8,128)(2,1)} %param.14) | data formatting | bytes 9437184 | tf_op args[5]
  36.2 6.8 %copy.16 = bf16[2048,1152]{0,1:T(8,128)(2,1)} copy(bf16[2048,1152]{1,0:T(8,128)(2,1)} %param.15) | data formatting | bytes 9437184 | tf_op args[6]
  43.0 0.0 copy-done.8
  43.0 0.1 reshape.43.stokes_ref
  43.1 14.2 %all-to-all-done.1 = bf16[16,72,512]{2,1,0:T(8,128)(2,1)S(1)} async-done(((bf16[16,72,512]{2,1,0:T(8,128)(2,1)}), bf16[16,72,512]{2,1,0:T(8,128)(2,1)S(1)}, u32[]{:S(2)}, u32[]{:S(2)}) %all-to-all-start.1) | async-done | bytes 1179680 | tf_op jit(solution)/shard_map/all_to_all | solution.py:253
  57.3 2.3 %copy-done = bf16[1152,2048]{0,1:T(8,128)(2,1)S(1)} copy-done((bf16[1152,2048]{0,1:T(8,128)(2,1)S(1)}, bf16[1152,2048]{0,1:T(8,128)(2,1)}, u32[]{:S(2)}) %copy-start) | copy-done | bytes 4718616
  59.6 2.3 %copy-done.2 = bf16[2048,1152]{0,1:T(8,128)(2,1)S(1)} copy-done((bf16[2048,1152]{0,1:T(8,128)(2,1)S(1)}, bf16[2048,1152]{0,1:T(8,128)(2,1)}, u32[]{:S(2)}) %copy-start.2) | copy-done | bytes 4718616
  61.9 6.9 %first_step.1 = (bf16[1152,256]{1,0:T(8,128)(2,1)}, bf16[1152,256]{1,0:T(8,128)(2,1)}, f32[2,75,512]{2,1,0:T(8,128)S(1)}) custom-call(bf16[1152,512]{1,0:T(8,128)(2,1)S(1)} %bitcast.27, bf16[2048,1152]{1,0:T(8,128)(2,1)S(1)} %bitcast.23, bf16[1152,2048]{1,0:T(8,128)(2,1)S(1)} %bitcast.25, bf16[2,75,1152]{2,1,0:T(8,128)(2,1)S(1)} %reshape.43.stokes_ref), custom_call_target="tpu_custom_call" | custom-call | flops 4831838208 | bytes 9437184 | tf_op jit(solution)/shard_map/first_step/pallas_call | solution.py:123
  68.8 3.7 %collective-permute-start.2 = (bf16[1152,256]{1,0:T(8,128)(2,1)}, bf16[1152,256]{1,0:T(8,128)(2,1)}, u32[]{:S(2)}, u32[]{:S(2)}) collective-permute-start(bf16[1152,256]{1,0:T(8,128)(2,1)} %get-tuple-element.8.refs_2_), channel_id=1, source_target_pairs={{0,1},{1,2},{2,3},{3,4},{4,5},{5,6},{6,7},{7,8},{8,9},{9,10},{10,1... | collective-permute-start | bytes 1769480 | tf_op jit(solution)/shard_map/ppermute | solution.py:295
  72.5 1.9 %collective-permute-start.3 = (bf16[1152,256]{1,0:T(8,128)(2,1)}, bf16[1152,256]{1,0:T(8,128)(2,1)}, u32[]{:S(2)}, u32[]{:S(2)}) collective-permute-start(bf16[1152,256]{1,0:T(8,128)(2,1)} %get-tuple-element.9.refs_1_), channel_id=1, source_target_pairs={{1,0},{2,1},{3,2},{4,3},{5,4},{6,5},{7,6},{8,7},{9,8},{10,9},{11,1... | collective-permute-start | bytes 1769480 | tf_op jit(solution)/shard_map/ppermute | solution.py:296
  74.4 0.0 copy-done.7
  74.4 0.2 fusion.1
  74.7 4.5 %collective-permute-start = (f32[2,75,256]{2,1,0:T(8,128)S(1)}, f32[2,75,256]{2,1,0:T(8,128)S(1)}, u32[]{:S(2)}, u32[]{:S(2)}) collective-permute-start(f32[2,75,256]{2,1,0:T(8,128)S(1)} %bitcast.35), channel_id=1, source_target_pairs={{0,1},{1,2},{2,3},{3,4},{4,5},{5,6},{6,7},{7,8},{8,9},{9,10},{10,1... | collective-permute-start | bytes 460808 | tf_op jit(solution)/shard_map/ppermute | solution.py:278
  79.3 1.9 %collective-permute-start.1 = (f32[2,75,256]{2,1,0:T(8,128)S(1)}, f32[2,75,256]{2,1,0:T(8,128)S(1)}, u32[]{:S(2)}, u32[]{:S(2)}) collective-permute-start(f32[2,75,256]{2,1,0:T(8,128)S(1)} %bitcast.36), channel_id=1, source_target_pairs={{1,0},{2,1},{3,2},{4,3},{5,4},{6,5},{7,6},{8,7},{9,8},{10,9},{11,1... | collective-permute-start | bytes 460808 | tf_op jit(solution)/shard_map/ppermute | solution.py:279
  81.2 0.2 reshape.52.ocean_ref
  81.5 0.1 multiply_sine_fusion
  81.5 0.1 broadcast_bitcast_fusion
  81.6 0.0 copy-done.9
  81.6 0.0 collective-permute-done.above_ref
  81.6 5.2 %collective-permute-done.1.below_ref = f32[2,75,256]{2,1,0:T(8,128)S(1)} collective-permute-done((f32[2,75,256]{2,1,0:T(8,128)S(1)}, f32[2,75,256]{2,1,0:T(8,128)S(1)}, u32[]{:S(2)}, u32[]{:S(2)}) %collective-permute-start.1) | collective-permute-done | bytes 153632 | tf_op jit(solution)/shard_map/ppermute | solution.py:279
  86.8 0.0 copy-done.5
  86.8 0.6 ocean_step.2.ocean_ref
  87.4 0.0 collective-permute-done.2.refs_0_
  87.4 0.0 collective-permute-done.3.refs_3_
  87.4 0.0 copy-start.1
  87.4 2.3 %copy-done.1 = bf16[1152,2048]{0,1:T(8,128)(2,1)S(1)} copy-done((bf16[1152,2048]{0,1:T(8,128)(2,1)S(1)}, bf16[1152,2048]{0,1:T(8,128)(2,1)}, u32[]{:S(2)}) %copy-start.1) | copy-done | bytes 4718616
  89.7 2.3 %copy-done.3 = bf16[2048,1152]{0,1:T(8,128)(2,1)S(1)} copy-done((bf16[2048,1152]{0,1:T(8,128)(2,1)S(1)}, bf16[2048,1152]{0,1:T(8,128)(2,1)}, u32[]{:S(2)}) %copy-start.3) | copy-done | bytes 4718616
  92.1 19.8 %second_step.1 = (bf16[1152,512]{1,0:T(8,128)(2,1)}, f32[2,75,512]{2,1,0:T(8,128)S(1)}) custom-call(bf16[2048,1152]{1,0:T(8,128)(2,1)S(1)} %bitcast.24, bf16[1152,2048]{1,0:T(8,128)(2,1)S(1)} %bitcast.26, bf16[2,75,1152]{2,1,0:T(8,128)(2,1)S(1)} %reshape.43.stokes_ref, f32[2,1152,128]{2,1,0:T(8,128)S(1)} %broadcast_in_dim.8.drift_ref, ...), custom_call_target="tpu_custom_call" | custom-call | flops 4831838208 | bytes 9437184 | tf_op jit(solution)/shard_map/second_step/pallas_call | solution.py:161
  111.9 8.1 %all-to-all-start.2 = ((bf16[16,72,512]{2,1,0:T(8,128)(2,1)}), bf16[16,72,512]{2,1,0:T(8,128)(2,1)S(1)}, u32[]{:S(2)}, u32[]{:S(2)}) async-start(bf16[16,72,512]{2,1,0:T(8,128)(2,1)} %bitcast.7), calls=%async_computation.2 | async-start | bytes 2359296 | tf_op jit(solution)/shard_map/all_to_all | solution.py:253
  120.0 3.4 %collective-permute-start.4 = (f32[2,75,256]{2,1,0:T(8,128)S(1)}, f32[2,75,256]{2,1,0:T(8,128)S(1)}, u32[]{:S(2)}, u32[]{:S(2)}) collective-permute-start(f32[2,75,256]{2,1,0:T(8,128)S(1)} %get-tuple-element.15), channel_id=1, source_target_pairs={{0,1},{1,2},{2,3},{3,4},{4,5},{5,6},{6,7},{7,8},{8,9},{9,10},{10,1... | collective-permute-start | bytes 460808 | tf_op jit(solution)/shard_map/ppermute | solution.py:300
  123.4 1.9 %collective-permute-start.5 = (f32[2,75,256]{2,1,0:T(8,128)S(1)}, f32[2,75,256]{2,1,0:T(8,128)S(1)}, u32[]{:S(2)}, u32[]{:S(2)}) collective-permute-start(f32[2,75,256]{2,1,0:T(8,128)S(1)} %get-tuple-element.14), channel_id=1, source_target_pairs={{1,0},{2,1},{3,2},{4,3},{5,4},{6,5},{7,6},{8,7},{9,8},{10,9},{11,1... | collective-permute-start | bytes 460808 | tf_op jit(solution)/shard_map/ppermute | solution.py:301
  125.3 22.5 %collective-permute-done.4.above_ref = f32[2,75,256]{2,1,0:T(8,128)S(1)} collective-permute-done((f32[2,75,256]{2,1,0:T(8,128)S(1)}, f32[2,75,256]{2,1,0:T(8,128)S(1)}, u32[]{:S(2)}, u32[]{:S(2)}) %collective-permute-start.4) | collective-permute-done | bytes 153632 | tf_op jit(solution)/shard_map/ppermute | solution.py:300
  147.8 1.7 %collective-permute-done.5.below_ref = f32[2,75,256]{2,1,0:T(8,128)S(1)} collective-permute-done((f32[2,75,256]{2,1,0:T(8,128)S(1)}, f32[2,75,256]{2,1,0:T(8,128)S(1)}, u32[]{:S(2)}, u32[]{:S(2)}) %collective-permute-start.5) | collective-permute-done | bytes 153632 | tf_op jit(solution)/shard_map/ppermute | solution.py:301
  149.5 0.6 ocean_step.3
  150.0 0.9 reshape.53
  150.9 0.0 all-to-all-done.2.parts_ref
  150.9 3.7 %gather_rows.1 = bf16[72,32,256]{2,1,0:T(8,128)(2,1)} custom-call(bf16[16,72,512]{2,1,0:T(8,128)(2,1)S(1)} %all-to-all-done.2.parts_ref), custom_call_target="tpu_custom_call" | custom-call | flops 589824 | bytes 2359296 | tf_op jit(solution)/shard_map/gather_rows/pallas_call | solution.py:235
  (14 shorter events, 0.1 us)
Async XLA Ops:
  0.6 13.3 %copy-start.6 = (s32[32,256]{1,0:T(8,128)S(1)}, s32[32,256]{1,0:T(8,128)}, u32[]{:S(2)}) copy-start(s32[32,256]{1,0:T(8,128)} %land_ref.1) | copy-start | bytes 98308
  0.6 13.3 %copy-start.4 = (bf16[72,32,256]{2,1,0:T(8,128)(2,1)S(1)}, bf16[72,32,256]{2,1,0:T(8,128)(2,1)}, u32[]{:S(2)}) copy-start(bf16[72,32,256]{2,1,0:T(8,128)(2,1)} %spec_ref.1) | copy-start | bytes 3538948
  2.1 10.8 %all-to-all-start = ((f32[16,2,2,256]{3,2,1,0:T(2,128)}), f32[16,2,2,256]{3,2,1,0:T(2,128)S(1)}, u32[]{:S(2)}, u32[]{:S(2)}) async-start(f32[16,2,2,256]{3,2,1,0:T(2,128)} %broadcast_in_dim.10), calls=%async_computation | async-start | bytes 131072 | tf_op jit(solution)/shard_map/all_to_all | solution.py:253
  23.2 34.0 %all-to-all-start.1 = ((bf16[16,72,512]{2,1,0:T(8,128)(2,1)}), bf16[16,72,512]{2,1,0:T(8,128)(2,1)S(1)}, u32[]{:S(2)}, u32[]{:S(2)}) async-start(bf16[16,72,512]{2,1,0:T(8,128)(2,1)} %move_bins.1), calls=%async_computation.1 | async-start | bytes 2359296 | tf_op jit(solution)/shard_map/all_to_all | solution.py:253
  36.2 6.8 %copy-start.8 = (bf16[150,1152]{1,0:T(8,128)(2,1)S(1)}, bf16[150,1152]{1,0:T(8,128)(2,1)}, u32[]{:S(2)}) copy-start(bf16[150,1152]{1,0:T(8,128)(2,1)} %param.16) | copy-start | bytes 1036804
  57.3 2.3 %copy-start = (bf16[1152,2048]{0,1:T(8,128)(2,1)S(1)}, bf16[1152,2048]{0,1:T(8,128)(2,1)}, u32[]{:S(2)}) copy-start(bf16[1152,2048]{0,1:T(8,128)(2,1)} %copy.15) | copy-start | bytes 14155780
  59.6 2.3 %copy-start.2 = (bf16[2048,1152]{0,1:T(8,128)(2,1)S(1)}, bf16[2048,1152]{0,1:T(8,128)(2,1)}, u32[]{:S(2)}) copy-start(bf16[2048,1152]{0,1:T(8,128)(2,1)} %copy.16) | copy-start | bytes 14155780
  61.9 12.5 %copy-start.7 = (f32[2,75,2,256]{3,2,1,0:T(2,128)S(1)}, f32[2,75,2,256]{3,2,1,0:T(2,128)}, u32[]{:S(2)}) copy-start(f32[2,75,2,256]{3,2,1,0:T(2,128)} %param.10) | copy-start | bytes 921604
  68.8 12.8 %copy-start.9 = (f32[2,2,256]{2,1,0:T(2,128)S(1)}, f32[2,2,256]{2,1,0:T(2,128)}, u32[]{:S(2)}) copy-start(f32[2,2,256]{2,1,0:T(2,128)} %param.11) | copy-start | bytes 12292
  68.8 18.0 %copy-start.5 = (f32[75,75]{1,0:T(8,128)S(1)}, f32[75,75]{1,0:T(8,128)}, u32[]{:S(2)}) copy-start(f32[75,75]{1,0:T(8,128)} %inverse_ref.3) | copy-start | bytes 67504
  68.8 18.6 %collective-permute-start.2 = (bf16[1152,256]{1,0:T(8,128)(2,1)}, bf16[1152,256]{1,0:T(8,128)(2,1)}, u32[]{:S(2)}, u32[]{:S(2)}) collective-permute-start(bf16[1152,256]{1,0:T(8,128)(2,1)} %get-tuple-element.8.refs_2_), channel_id=1, source_target_pairs={{0,1},{1,2},{2,3},{3,4},{4,5},{5,6},{6,7},{7,8},{8,9},{9,10},{10,1... | collective-permute-start | bytes 1769480 | tf_op jit(solution)/shard_map/ppermute | solution.py:295
  72.5 14.9 %collective-permute-start.3 = (bf16[1152,256]{1,0:T(8,128)(2,1)}, bf16[1152,256]{1,0:T(8,128)(2,1)}, u32[]{:S(2)}, u32[]{:S(2)}) collective-permute-start(bf16[1152,256]{1,0:T(8,128)(2,1)} %get-tuple-element.9.refs_1_), channel_id=1, source_target_pairs={{1,0},{2,1},{3,2},{4,3},{5,4},{6,5},{7,6},{8,7},{9,8},{10,9},{11,1... | collective-permute-start | bytes 1769480 | tf_op jit(solution)/shard_map/ppermute | solution.py:296
  74.7 6.9 %collective-permute-start = (f32[2,75,256]{2,1,0:T(8,128)S(1)}, f32[2,75,256]{2,1,0:T(8,128)S(1)}, u32[]{:S(2)}, u32[]{:S(2)}) collective-permute-start(f32[2,75,256]{2,1,0:T(8,128)S(1)} %bitcast.35), channel_id=1, source_target_pairs={{0,1},{1,2},{2,3},{3,4},{4,5},{5,6},{6,7},{7,8},{8,9},{9,10},{10,1... | collective-permute-start | bytes 460808 | tf_op jit(solution)/shard_map/ppermute | solution.py:278
  79.3 7.5 %collective-permute-start.1 = (f32[2,75,256]{2,1,0:T(8,128)S(1)}, f32[2,75,256]{2,1,0:T(8,128)S(1)}, u32[]{:S(2)}, u32[]{:S(2)}) collective-permute-start(f32[2,75,256]{2,1,0:T(8,128)S(1)} %bitcast.36), channel_id=1, source_target_pairs={{1,0},{2,1},{3,2},{4,3},{5,4},{6,5},{7,6},{8,7},{9,8},{10,9},{11,1... | collective-permute-start | bytes 460808 | tf_op jit(solution)/shard_map/ppermute | solution.py:279
  87.4 2.3 %copy-start.1 = (bf16[1152,2048]{0,1:T(8,128)(2,1)S(1)}, bf16[1152,2048]{0,1:T(8,128)(2,1)}, u32[]{:S(2)}) copy-start(bf16[1152,2048]{0,1:T(8,128)(2,1)} %copy.15) | copy-start | bytes 14155780
  89.7 2.3 %copy-start.3 = (bf16[2048,1152]{0,1:T(8,128)(2,1)S(1)}, bf16[2048,1152]{0,1:T(8,128)(2,1)}, u32[]{:S(2)}) copy-start(bf16[2048,1152]{0,1:T(8,128)(2,1)} %copy.16) | copy-start | bytes 14155780
  111.9 39.0 %all-to-all-start.2 = ((bf16[16,72,512]{2,1,0:T(8,128)(2,1)}), bf16[16,72,512]{2,1,0:T(8,128)(2,1)S(1)}, u32[]{:S(2)}, u32[]{:S(2)}) async-start(bf16[16,72,512]{2,1,0:T(8,128)(2,1)} %bitcast.7), calls=%async_computation.2 | async-start | bytes 2359296 | tf_op jit(solution)/shard_map/all_to_all | solution.py:253
  120.0 27.8 %collective-permute-start.4 = (f32[2,75,256]{2,1,0:T(8,128)S(1)}, f32[2,75,256]{2,1,0:T(8,128)S(1)}, u32[]{:S(2)}, u32[]{:S(2)}) collective-permute-start(f32[2,75,256]{2,1,0:T(8,128)S(1)} %get-tuple-element.15), channel_id=1, source_target_pairs={{0,1},{1,2},{2,3},{3,4},{4,5},{5,6},{6,7},{7,8},{8,9},{9,10},{10,1... | collective-permute-start | bytes 460808 | tf_op jit(solution)/shard_map/ppermute | solution.py:300
  123.4 26.1 %collective-permute-start.5 = (f32[2,75,256]{2,1,0:T(8,128)S(1)}, f32[2,75,256]{2,1,0:T(8,128)S(1)}, u32[]{:S(2)}, u32[]{:S(2)}) collective-permute-start(f32[2,75,256]{2,1,0:T(8,128)S(1)} %get-tuple-element.14), channel_id=1, source_target_pairs={{1,0},{2,1},{3,2},{4,3},{5,4},{6,5},{7,6},{8,7},{9,8},{10,9},{11,1... | collective-permute-start | bytes 460808 | tf_op jit(solution)/shard_map/ppermute | solution.py:301

commit v2 on v1

--- a/solution.py
+++ b/solution.py
@@ -32,40 +32,42 @@
     return jnp.concatenate([part] * (cols // part.shape[1]), axis=1)
 
 
+PAD = 8
+
+
 def move_bins_kernel(me_ref, spec_ref, ocean_ref, land_ref, drift_ref, out_ref, *planes):
     bins, rows, cols = spec_ref.shape
     devices, _, row_dev, _ = ocean_ref.shape
+    pitch = rows + PAD
     first = pl.multiple_of(me_ref[0] * bins, 8)
 
-    @pl.loop(0, bins)
+    @pl.loop(0, bins, unroll=8)
     def _(b):
         plane = spec_ref[b].astype(jnp.float32)
         for h, ref in enumerate(planes):
-            ref[pl.ds(b * rows, rows), :] = plane[:, h * 128 : (h + 1) * 128]
+            ref[pl.ds(pl.multiple_of(b * pitch, 8), rows), :] = plane[:, h * 128 : (h + 1) * 128]
 
     size = 24 if bins % 24 == 0 else 8
 
     def row(b, r):
-        return jnp.concatenate(
-            [ref[pl.ds(b * rows + r, size, stride=rows), :] for ref in planes], axis=1
-        )
-
-    @pl.loop(0, devices)
+        at = pl.ds(b * pitch + r, size, stride=pitch)
+        return jnp.concatenate([ref[at, :] for ref in planes], axis=1)
+
+    @pl.loop(0, devices, unroll=2)
     def _(d):
-        for j in range(row_dev):
-            r = d * row_dev + j
-            land = land_ref[pl.ds(r, 1), :].astype(jnp.float32)
-            east, north = (ocean_ref[d, s, j : j + 1, :] for s in range(2))
-            for b in range(0, bins, size):
-                f = row(b, r)
-                above = row(b, jnp.maximum(r - 1, 0))
-                below = row(b, jnp.minimum(r + 1, rows - 1))
-                above = jnp.where(r > 0, above, 0.0)
-                below = jnp.where(r < rows - 1, below, 0.0)
-                here = pl.ds(pl.multiple_of(first + b, 8), size)
-                moved = upwind(
-                    f, above, below, wide(drift_ref, 0, here, cols), wide(drift_ref, 1, here, cols), east, north, land
-                )
+        low = d * row_dev
+        for b in range(0, bins, size):
+            here = pl.ds(pl.multiple_of(first + b, 8), size)
+            drift_x, drift_y = (wide(drift_ref, s, here, cols) for s in range(2))
+            field = [row(b, jnp.maximum(low - 1, 0))]
+            field += [row(b, low + j) for j in range(row_dev)]
+            field += [row(b, jnp.minimum(low + row_dev, rows - 1))]
+            field[0] = jnp.where(d > 0, field[0], 0.0)
+            field[-1] = jnp.where(d < devices - 1, field[-1], 0.0)
+            for j in range(row_dev):
+                land = land_ref[pl.ds(low + j, 1), :].astype(jnp.float32)
+                east, north = (ocean_ref[d, s, j : j + 1, :] for s in range(2))
+                moved = upwind(field[j + 1], field[j], field[j + 2], drift_x, drift_y, east, north, land)
                 out_ref[d, b : b + size, j * cols : (j + 1) * cols] = moved.astype(jnp.bfloat16)
 
 
@@ -77,69 +79,121 @@
         out_shape=jax.ShapeDtypeStruct((devices, bins, row_dev * cols), jnp.bfloat16),
         in_specs=[pl.BlockSpec(memory_space=pltpu.SMEM)] + [VMEM] * 4,
         out_specs=VMEM,
-        scratch_shapes=[pltpu.VMEM((bins * rows, 128), jnp.float32)] * (cols // 128),
+        scratch_shapes=[pltpu.VMEM((bins * (rows + PAD), 128), jnp.float32)] * (cols // 128),
         compiler_params=pltpu.CompilerParams(vmem_limit_bytes=20 * 1024 * 1024),
         cost_estimate=pl.CostEstimate(flops=40 * spectrum.size, bytes_accessed=4 * spectrum.size, transcendentals=2 * spectrum.size),
         name="move_bins",
     )(me, spectrum, ocean_top, land_mask, drift)
 
 
+def turn_kernel(step, win_ref, wout_ref, win_t, wout_t, win_buf, wout_buf, sems):
+    jobs = []
+    for n, (source, target, buf) in enumerate(((win_ref, win_t, win_buf), (wout_ref, wout_t, wout_buf))):
+        for i in range(source.shape[1] // step):
+            lanes = slice(i * step, (i + 1) * step)
+            copy = pltpu.make_async_copy(source.at[:, lanes], buf.at[i % 2], sems.at[n, i % 2])
+            jobs.append((copy, target, lanes, buf, i % 2))
+    jobs[0][0].start()
+    for k, (copy, target, lanes, buf, slot) in enumerate(jobs):
+        if k + 1 < len(jobs):
+            jobs[k + 1][0].start()
+        copy.wait()
+        target[lanes, :] = buf[slot].T
+
+
+def turn_weights(coupling_in, coupling_out):
+    step = 128
+    return pl.pallas_call(
+        functools.partial(turn_kernel, step),
+        out_shape=[jax.ShapeDtypeStruct(w.shape[::-1], w.dtype) for w in (coupling_in, coupling_out)],
+        in_specs=[pl.BlockSpec(memory_space=pl.ANY)] * 2,
+        out_specs=[VMEM] * 2,
+        scratch_shapes=[pltpu.VMEM((2, w.shape[0], step), w.dtype) for w in (coupling_in, coupling_out)]
+        + [pltpu.SemaphoreType.DMA((2, 2))],
+        compiler_params=pltpu.CompilerParams(vmem_limit_bytes=8 * 1024 * 1024),
+        cost_estimate=pl.CostEstimate(flops=0, bytes_accessed=8 * coupling_in.size, transcendentals=0),
+        name="turn_weights",
+    )(coupling_in, coupling_out)
+
+
 def tile_of(total, most):
     return next(t for t in range(most - most % 8, 0, -8) if total % t == 0)
 
 
-def interact_body(moved_ref, win_ref, wout_ref, stokes_ref, active, updated_refs, whole, profile_ref, tk, tm):
-    terms_count, bins = win_ref.shape
-
-    @pl.loop(0, terms_count // tk)
-    def _(i):
-        at = pl.ds(pl.multiple_of(i * tk, tk), tk)
-        terms = jnp.dot(win_ref[at, :], moved_ref[...], preferred_element_type=jnp.float32)
+def weight_copies(refs, buffers, sems):
+    copies = []
+    for n, (ref, buffer) in enumerate(zip(refs, buffers)):
+        tile = ref.shape[0] // sems.shape[1]
+        rows = [pl.ds(i * tile, tile) for i in range(sems.shape[1])]
+        copies.append([(at, pltpu.make_async_copy(ref.at[at, :], buffer.at[at, :], sems.at[n, i])) for i, at in enumerate(rows)])
+    for group in copies:
+        for _, copy in group:
+            copy.start()
+    return copies
+
+
+def interact_body(copies, buffers, moved_ref, active, updated_refs):
+    win, wout = buffers
+    for at, copy in copies[0]:
+        copy.wait()
+        terms = jnp.dot(win[at, :], moved_ref[...], preferred_element_type=jnp.float32)
         active[at, :] = (terms * jnp.tanh(terms)).astype(jnp.bfloat16)
-
-    @pl.loop(0, bins // tm)
-    def _(i):
-        at = pl.ds(pl.multiple_of(i * tm, 8), tm)
-        source = jnp.dot(wout_ref[at, :], active[...], preferred_element_type=jnp.float32)
+    for at, copy in copies[1]:
+        copy.wait()
+        source = jnp.dot(wout[at, :], active[...], preferred_element_type=jnp.float32)
         updated = (moved_ref[at, :].astype(jnp.float32) + source).astype(jnp.bfloat16)
-        whole[at, :] = updated
-        width = updated.shape[1] // max(1, len(updated_refs))
+        width = updated.shape[1] // len(updated_refs)
         for j, ref in enumerate(updated_refs):
             ref[at, :] = updated[:, j * width : (j + 1) * width]
 
-    for s in range(2):
-        profile_ref[s] = jnp.dot(stokes_ref[s], whole[...], preferred_element_type=jnp.float32)
-
-
-def first_kernel(moved_ref, win_ref, wout_ref, stokes_ref, *refs):
-    *updated_refs, profile_ref, active, whole = refs
-    tk, tm = tile_of(win_ref.shape[0], 1024), tile_of(wout_ref.shape[0], 576)
-    interact_body(moved_ref, win_ref, wout_ref, stokes_ref, active, updated_refs, whole, profile_ref, tk, tm)
-
-
-def first_step(moved, win, wout, stokes, row_dev):
+
+def weight_scratch(win, wout, points):
+    pieces = 4
+    return [
+        pltpu.VMEM(win.shape, win.dtype),
+        pltpu.VMEM(wout.shape, wout.dtype),
+        pltpu.VMEM((win.shape[0], points), jnp.bfloat16),
+        pltpu.SemaphoreType.DMA((2, pieces)),
+    ]
+
+
+ANY = pl.BlockSpec(memory_space=pl.ANY)
+
+
+def in_hbm(*arrays):
+    return [pltpu.with_memory_space_constraint(x, pltpu.HBM) for x in arrays]
+
+
+def first_kernel(moved_ref, win_ref, wout_ref, *refs):
+    *updated_refs, win, wout, active, sems = refs
+    copies = weight_copies((win_ref, wout_ref), (win, wout), sems)
+    interact_body(copies, (win, wout), moved_ref, active, updated_refs)
+
+
+def first_step(moved, win, wout, row_dev):
     bins, points = moved.shape
-    terms, levels = win.shape[0], stokes.shape[1]
+    terms = win.shape[0]
     return pl.pallas_call(
         first_kernel,
-        out_shape=[jax.ShapeDtypeStruct((bins, points // row_dev), jnp.bfloat16)] * row_dev
-        + [jax.ShapeDtypeStruct((2, levels, points), jnp.float32)],
-        in_specs=[VMEM] * 4,
-        out_specs=[VMEM] * (row_dev + 1),
-        scratch_shapes=[pltpu.VMEM((terms, points), jnp.bfloat16), pltpu.VMEM((bins, points), jnp.bfloat16)],
-        compiler_params=pltpu.CompilerParams(vmem_limit_bytes=24 * 1024 * 1024),
+        out_shape=[jax.ShapeDtypeStruct((bins, points // row_dev), jnp.bfloat16)] * row_dev,
+        in_specs=[VMEM, ANY, ANY],
+        out_specs=[VMEM] * row_dev,
+        scratch_shapes=weight_scratch(win, wout, points),
+        compiler_params=pltpu.CompilerParams(vmem_limit_bytes=28 * 1024 * 1024),
         cost_estimate=pl.CostEstimate(flops=4 * bins * terms * points, bytes_accessed=4 * bins * terms, transcendentals=terms * points),
         name="first_step",
-    )(moved, win, wout, stokes)
-
-
-def second_kernel(win_ref, wout_ref, stokes_ref, drift_ref, ocean_ref, land_ref, *refs):
-    *row_refs, whole, profile_ref, active, moved = refs
+    )(moved, *in_hbm(win, wout))
+
+
+def second_kernel(win_ref, wout_ref, drift_ref, ocean_ref, land_ref, *refs):
+    *row_refs, whole, win, wout, active, sems, moved = refs
+    copies = weight_copies((win_ref, wout_ref), (win, wout), sems)
     bins, cols = row_refs[0].shape
     row_dev = len(row_refs) - 2
     size = 16
-
-    @pl.loop(0, bins // size)
+    count = bins // size
+
+    @pl.loop(0, count, unroll=8 if count % 8 == 0 else 1)
     def _(i):
         at = pl.ds(pl.multiple_of(i * size, size), size)
         rows = [ref[at, :].astype(jnp.float32) for ref in row_refs]
@@ -150,30 +204,27 @@
             new = upwind(rows[j + 1], rows[j], rows[j + 2], drift_x, drift_y, east, north, land_ref[:, lanes])
             moved[at, lanes] = new.astype(jnp.bfloat16)
 
-    tk, tm = tile_of(win_ref.shape[0], 1024), tile_of(wout_ref.shape[0], 576)
-    interact_body(moved, win_ref, wout_ref, stokes_ref, active, (), whole, profile_ref, tk, tm)
-
-
-def second_step(rows, win, wout, stokes, drift, ocean, land):
+    interact_body(copies, (win, wout), moved, active, (whole,))
+
+
+def second_step(rows, win, wout, drift, ocean, land):
     bins, cols = rows[0].shape
     points = cols * (len(rows) - 2)
-    terms, levels = win.shape[0], stokes.shape[1]
+    terms = win.shape[0]
     return pl.pallas_call(
         second_kernel,
-        out_shape=[
-            jax.ShapeDtypeStruct((bins, points), jnp.bfloat16),
-            jax.ShapeDtypeStruct((2, levels, points), jnp.float32),
-        ],
-        in_specs=[VMEM] * (6 + len(rows)),
-        out_specs=[VMEM] * 2,
-        scratch_shapes=[pltpu.VMEM((terms, points), jnp.bfloat16), pltpu.VMEM((bins, points), jnp.bfloat16)],
-        compiler_params=pltpu.CompilerParams(vmem_limit_bytes=24 * 1024 * 1024),
+        out_shape=jax.ShapeDtypeStruct((bins, points), jnp.bfloat16),
+        in_specs=[ANY, ANY] + [VMEM] * (3 + len(rows)),
+        out_specs=VMEM,
+        scratch_shapes=weight_scratch(win, wout, points) + [pltpu.VMEM((bins, points), jnp.bfloat16)],
+        compiler_params=pltpu.CompilerParams(vmem_limit_bytes=28 * 1024 * 1024),
         cost_estimate=pl.CostEstimate(flops=4 * bins * terms * points, bytes_accessed=4 * bins * terms, transcendentals=terms * points),
         name="second_step",
-    )(win, wout, stokes, drift, ocean, land, *rows)
-
-
-def ocean_kernel(ocean_ref, above_ref, below_ref, profile_ref, wind_ref, inverse_ref, land_ref, latitude_ref, out_ref):
+    )(*in_hbm(win, wout), drift, ocean, land, *rows)
+
+
+def ocean_kernel(ocean_ref, above_ref, below_ref, stokes_ref, wind_ref, inverse_ref, land_ref, latitude_ref, *refs):
+    *wave_refs, out_ref = refs
     levels, points = ocean_ref.shape[1:]
     cols = above_ref.shape[2]
     row_dev = points // cols
@@ -181,7 +232,10 @@
     top = lax.broadcasted_iota(jnp.int32, (levels, points), 0) == 0
     for s in range(2):
         center = ocean_ref[s]
-        other = ocean_ref[1 - s] + profile_ref[1 - s]
+        drift = [
+            jnp.dot(stokes_ref[1 - s], ref[...], preferred_element_type=jnp.float32) for ref in wave_refs
+        ]
+        other = ocean_ref[1 - s] + (drift[0] if len(drift) == 1 else jnp.concatenate(drift, axis=1))
         pieces = [center[:, j * cols : (j + 1) * cols] for j in range(row_dev)]
         rows = [above_ref[s]] + pieces + [below_ref[s]]
         around = [
@@ -196,22 +250,22 @@
         out_ref[s] = mixed * land_ref[...]
 
 
-def ocean_step(ocean, above, below, profile, wind, inverse, land, latitude):
+def ocean_step(ocean, above, below, stokes, wind, inverse, land, latitude, waves):
     return pl.pallas_call(
         ocean_kernel,
         out_shape=jax.ShapeDtypeStruct(ocean.shape, jnp.float32),
-        in_specs=[VMEM] * 8,
+        in_specs=[VMEM] * (8 + len(waves)),
         out_specs=VMEM,
         compiler_params=pltpu.CompilerParams(vmem_limit_bytes=8 * 1024 * 1024),
         cost_estimate=pl.CostEstimate(flops=12 * inverse.shape[0] * ocean.size, bytes_accessed=12 * ocean.size, transcendentals=0),
         name="ocean_step",
-    )(ocean, above, below, profile, wind, inverse, land, latitude)
+    )(ocean, above, below, stokes, wind, inverse, land, latitude, *waves)
 
 
 def gather_kernel(parts_ref, out_ref, *planes):
     devices, bins, points = parts_ref.shape
     rows, cols = out_ref.shape[1:]
-    row_dev = rows // devices
+    row_dev, pitch = rows // devices, rows + PAD
     size = 24 if bins % 24 == 0 else 8
 
     @pl.loop(0, devices)
@@ -219,15 +273,15 @@
         for b in range(0, bins, size):
             part = parts_ref[d, b : b + size, :].astype(jnp.float32)
             for j in range(row_dev):
-                at = pl.ds(b * rows + d * row_dev + j, size, stride=rows)
+                at = pl.ds(b * pitch + d * row_dev + j, size, stride=pitch)
                 for h, ref in enumerate(planes):
                     low = j * cols + h * 128
                     ref[at, :] = part[:, low : low + 128]
 
-    @pl.loop(0, bins)
+    @pl.loop(0, bins, unroll=8)
     def _(b):
-        plane = [ref[pl.ds(b * rows, rows), :] for ref in planes]
-        out_ref[b] = jnp.concatenate(plane, axis=1).astype(jnp.bfloat16)
+        at = pl.ds(pl.multiple_of(b * pitch, 8), rows)
+        out_ref[b] = jnp.concatenate([ref[at, :] for ref in planes], axis=1).astype(jnp.bfloat16)
 
 
 def gather_rows(parts, rows, cols):
@@ -237,7 +291,7 @@
         out_shape=jax.ShapeDtypeStruct((bins, rows, cols), jnp.bfloat16),
         in_specs=[VMEM],
         out_specs=VMEM,
-        scratch_shapes=[pltpu.VMEM((bins * rows, 128), jnp.float32)] * (cols // 128),
+        scratch_shapes=[pltpu.VMEM((bins * (rows + PAD), 128), jnp.float32)] * (cols // 128),
         compiler_params=pltpu.CompilerParams(vmem_limit_bytes=20 * 1024 * 1024),
         cost_estimate=pl.CostEstimate(flops=parts.size, bytes_accessed=4 * parts.size, transcendentals=0),
         name="gather_rows",
@@ -278,8 +332,6 @@
     ocean_above = lax.ppermute(ocean_currents[:, :, -1], "grid", up)
     ocean_below = lax.ppermute(ocean_currents[:, :, 0], "grid", down)
 
-    win = coupling_in.T
-    wout = coupling_out.T
     stokes = stokes_weight.reshape(2, levels, -1)
     drift = jnp.broadcast_to(bin_drift[:, :, None], bin_drift.shape + (128,))
     land = lax.dynamic_slice_in_dim(land_mask, device * row_dev, row_dev, 0)
@@ -290,16 +342,22 @@
     wind = wind_stress.reshape(2, points)
     ocean = ocean_currents.reshape(2, levels, points)
 
-    moved = exchange(move_bins(me, spectrum, tops, land_mask, drift))
-    *updated, profile = first_step(moved.reshape(-1, points), win, wout, stokes, row_dev)
+    moved = move_bins(me, spectrum, tops, land_mask, drift)
+    moved, coupling_in, coupling_out = lax.optimization_barrier((moved, coupling_in, coupling_out))
+    win, wout = turn_weights(*in_hbm(coupling_in, coupling_out))
+    moved = exchange(moved)
+    moved, win, wout, stokes, ocean_above, ocean_below, ocean, wind, land, latitude = lax.optimization_barrier(
+        (moved, win, wout, stokes, ocean_above, ocean_below, ocean, wind, land, latitude)
+    )
+    updated = first_step(moved.reshape(-1, points), win, wout, row_dev)
     above = lax.ppermute(updated[-1], "grid", up)
     below = lax.ppermute(updated[0], "grid", down)
-    ocean = ocean_step(ocean, ocean_above, ocean_below, profile, wind, mixing_inverse, land, latitude)
-    whole, profile = second_step([above, *updated, below], win, wout, stokes, drift, ocean, land)
+    ocean = ocean_step(ocean, ocean_above, ocean_below, stokes, wind, mixing_inverse, land, latitude, updated)
+    whole = second_step([above, *updated, below], win, wout, drift, ocean, land)
     spectra = exchange(whole.reshape(devices, bins, points))
     ocean_above = lax.ppermute(ocean[:, :, -cols:], "grid", up)
     ocean_below = lax.ppermute(ocean[:, :, :cols], "grid", down)
-    ocean = ocean_step(ocean, ocean_above, ocean_below, profile, wind, mixing_inverse, land, latitude)
+    ocean = ocean_step(ocean, ocean_above, ocean_below, stokes, wind, mixing_inverse, land, latitude, [whole])
     return gather_rows(spectra, rows, cols), ocean.reshape(2, levels, row_dev, cols)
 
 

time: 156 us -> 129 us (0.83)
  local copies, waits for them, and re-layouts: 27 us -> 11.1 us
  waiting for transfers between devices: 47.7 us -> 39.4 us
  starting transfers between devices: 38.2 us -> 35.9 us
    unnamed x28 -> x20, local copies, waits for them, and re-layouts: 23 us -> 5.8 us
    all_to_all x3, waiting for transfers between devices: 18.4 us -> 4.29 us  [exchange(): lax.all_to_all(value, 'grid', split_axis=0, concat_axis=0, tiled=True)]
    pallas_call x1, Pallas kernels: 9.27 us -> 3.88 us  [move_bins(): pl.pallas_call(move_bins_kernel, out_shape=jax.ShapeDtypeStruct((devices,...]
    ppermute x1, waiting for transfers between devices: 0.01 us -> 5.25 us  [per_device(): below = lax.ppermute(updated[0], 'grid', down)]
    pallas_call x1 -> x2, Pallas kernels: 19.8 us -> 24.2 us  [the longest x1 14.1 us: turn_weights(): pl.pallas_call(functools.partial(turn_kernel, step), out_shape=[jax.Shape...]
    ppermute x1, waiting for transfers between devices: 5.17 us -> 1.58 us  [per_device(): ocean_below = lax.ppermute(ocean_currents[:, :, 0], 'grid', down)]
    ppermute x1, waiting for transfers between devices: 0.01 us -> 3.52 us  [per_device(): above = lax.ppermute(updated[-1], 'grid', up)]
    pallas_call x2, Pallas kernels: 1.13 us -> 3.52 us  [ocean_step(): pl.pallas_call(ocean_kernel, out_shape=jax.ShapeDtypeStruct(ocean.shape,...]
  transfers between devices with their start and end apart: 9 -> 9, of which waited for: 5 -> 7; matrix products, arithmetic and copies ran while one was open for 10% -> 3% of each run, Pallas kernels for 1% -> 14%
where the time goes in v2:
time: 129 us; the launch traced here: 128 us
  Pallas kernels  41.1 us (32%)
  waiting for transfers between devices  39.4 us (31%)
  starting transfers between devices  35.9 us (28%)
  local copies, waits for them, and re-layouts  11.1 us (9%)
    ppermute x1, waiting for transfers between devices, per_device(): ocean_above = lax.ppermute(ocean[:, :, -cols:], 'grid', up)  22.5 us
    all_to_all x3, starting transfers between devices, exchange(): lax.all_to_all(value, 'grid', split_axis=0, concat_axis=0, tiled=True)  19.5 us
    pallas_call x1, Pallas kernels, turn_weights(): pl.pallas_call(functools.partial(turn_kernel, step), out_shape=[jax.Shape...  14.1 us
    pallas_call x1, Pallas kernels, second_step(): pl.pallas_call(second_kernel, out_shape=jax.ShapeDtypeStruct((bins, point...  10.1 us
    pallas_call x1, Pallas kernels, first_step(): pl.pallas_call(first_kernel, out_shape=[jax.ShapeDtypeStruct((bins, point...  7.85 us
    unnamed x20, local copies, waits for them, and re-layouts  5.8 us
    ppermute x1, waiting for transfers between devices, per_device(): below = lax.ppermute(updated[0], 'grid', down)  5.25 us
    all_to_all x3, waiting for transfers between devices, exchange(): lax.all_to_all(value, 'grid', split_axis=0, concat_axis=0, tiled=True)  4.29 us
  transfers between devices with their start and end apart: 9, of which 7 were waited for; matrix products, arithmetic and copies ran while one was open for 3% of the time, Pallas kernels for 14%

profile of v2, /device:TPU:13, one launch (start us, length us, event | category | flops | bytes accessed | tf_op | source)
XLA Modules:
  0.0 128.4 jit_solution(1279421178917946607)
XLA Ops:
  0.6 0.0 copy-start.2
  0.6 0.0 copy-start
  0.6 0.8 slice_bitcast_fusion
  1.4 0.6 broadcast_in_dim.9
  2.1 6.5 %all-to-all-start = ((f32[16,2,2,256]{3,2,1,0:T(2,128)}), f32[16,2,2,256]{3,2,1,0:T(2,128)S(1)}, u32[]{:S(2)}, u32[]{:S(2)}) async-start(f32[16,2,2,256]{3,2,1,0:T(2,128)} %broadcast_in_dim.9), calls=%async_computation | async-start | bytes 131072 | tf_op jit(solution)/shard_map/all_to_all | solution.py:307
  8.6 4.3 %all-to-all-done.ocean_ref = f32[16,2,2,256]{3,2,1,0:T(2,128)S(1)} async-done(((f32[16,2,2,256]{3,2,1,0:T(2,128)}), f32[16,2,2,256]{3,2,1,0:T(2,128)S(1)}, u32[]{:S(2)}, u32[]{:S(2)}) %all-to-all-start) | async-done | bytes 65568 | tf_op jit(solution)/shard_map/all_to_all | solution.py:307
  12.9 1.1 broadcast_in_dim.10.drift_ref
  14.0 0.0 copy-done.2
  14.0 0.0 copy-done
  14.0 3.9 %move_bins.1 = bf16[16,72,512]{2,1,0:T(8,128)(2,1)} custom-call(s32[1]{0:T(128)} %bitcast.me_ref, bf16[72,32,256]{2,1,0:T(8,128)(2,1)S(1)} %copy-done, f32[16,2,2,256]{3,2,1,0:T(2,128)S(1)} %all-to-all-done.ocean_ref, s32[32,256]{1,0:T(8,128)S(1)} %copy-done.2, f32[2,1152,128]{2,1,0:T(8,128)S(1)} %broadcast_in_dim.10.drift_ref), custom_call_target="tpu_custom_call" | custom-call | flops 23592960 | bytes 2359296 | tf_op jit(solution)/shard_map/move_bins/pallas_call | solution.py:77
  17.9 6.3 %all-to-all-start.1 = ((bf16[16,72,512]{2,1,0:T(8,128)(2,1)}), bf16[16,72,512]{2,1,0:T(8,128)(2,1)S(1)}, u32[]{:S(2)}, u32[]{:S(2)}) async-start(bf16[16,72,512]{2,1,0:T(8,128)(2,1)} %move_bins.1), calls=%async_computation.1 | async-start | bytes 2359296 | tf_op jit(solution)/shard_map/all_to_all | solution.py:307
  24.2 0.0 copy-done.5
  24.2 0.2 fusion.1
  24.5 0.7 copy.29
  25.1 3.5 %collective-permute-start = (f32[2,75,256]{2,1,0:T(8,128)}, f32[2,75,256]{2,1,0:T(8,128)S(1)}, u32[]{:S(2)}, u32[]{:S(2)}) collective-permute-start(f32[2,75,256]{2,1,0:T(8,128)} %bitcast.20), channel_id=1, source_target_pairs={{0,1},{1,2},{2,3},{3,4},{4,5},{5,6},{6,7},{7,8},{8,9},{9,10},{10,1... | collective-permute-start | bytes 460808 | tf_op jit(solution)/shard_map/ppermute | solution.py:332
  28.6 0.7 copy.28
  29.3 1.9 %collective-permute-start.1 = (f32[2,75,256]{2,1,0:T(8,128)}, f32[2,75,256]{2,1,0:T(8,128)S(1)}, u32[]{:S(2)}, u32[]{:S(2)}) collective-permute-start(f32[2,75,256]{2,1,0:T(8,128)} %bitcast.19), channel_id=1, source_target_pairs={{1,0},{2,1},{3,2},{4,3},{5,4},{6,5},{7,6},{8,7},{9,8},{10,9},{11,1... | collective-permute-start | bytes 460808 | tf_op jit(solution)/shard_map/ppermute | solution.py:333
  31.3 0.2 reshape.52
  31.5 0.1 multiply_sine_fusion
  31.6 0.1 broadcast_bitcast_fusion
  31.7 0.2 copy.19
  31.9 1.1 reshape.44.stokes_ref
  33.0 0.0 copy-done.6
  33.0 14.1 %turn_weights.1 = (bf16[2048,1152]{1,0:T(8,128)(2,1)S(1)}, bf16[1152,2048]{1,0:T(8,128)(2,1)S(1)}) custom-call(bf16[1152,2048]{1,0:T(8,128)(2,1)} %win_ref, bf16[2048,1152]{1,0:T(8,128)(2,1)} %wout_ref), custom_call_target="tpu_custom_call" | custom-call | bytes 18874368 | tf_op jit(solution)/shard_map/turn_weights/pallas_call | solution.py:106
  47.1 0.0 copy-start.3
  47.1 2.1 %copy-done.3 = bf16[2048,1152]{1,0:T(8,128)(2,1)} copy-done((bf16[2048,1152]{1,0:T(8,128)(2,1)}, bf16[2048,1152]{1,0:T(8,128)(2,1)S(1)}, u32[]{:S(2)}) %copy-start.3) | copy-done | bytes 4718616
  49.2 2.2 %copy-done.4 = bf16[1152,2048]{1,0:T(8,128)(2,1)} copy-done((bf16[1152,2048]{1,0:T(8,128)(2,1)}, bf16[1152,2048]{1,0:T(8,128)(2,1)S(1)}, u32[]{:S(2)}) %copy-start.4) | copy-done | bytes 4718616
  51.4 0.7 collective-permute-done.above_ref
  52.1 1.6 %collective-permute-done.1.below_ref = f32[2,75,256]{2,1,0:T(8,128)S(1)} collective-permute-done((f32[2,75,256]{2,1,0:T(8,128)}, f32[2,75,256]{2,1,0:T(8,128)S(1)}, u32[]{:S(2)}, u32[]{:S(2)}) %collective-permute-start.1) | collective-permute-done | bytes 153632 | tf_op jit(solution)/shard_map/ppermute | solution.py:333
  53.7 0.0 all-to-all-done.1
  53.7 7.9 %first_step.1 = (bf16[1152,256]{1,0:T(8,128)(2,1)S(1)}, bf16[1152,256]{1,0:T(8,128)(2,1)S(1)}) custom-call(bf16[1152,512]{1,0:T(8,128)(2,1)S(1)} %bitcast.21, bf16[2048,1152]{1,0:T(8,128)(2,1)} %copy-done.3, bf16[1152,2048]{1,0:T(8,128)(2,1)} %copy-done.4), custom_call_target="tpu_custom_call" | custom-call | flops 4831838208 | bytes 9437184 | tf_op jit(solution)/shard_map/first_step/pallas_call | solution.py:176
  61.5 3.6 %collective-permute-start.2 = (bf16[1152,256]{1,0:T(8,128)(2,1)S(1)}, bf16[1152,256]{1,0:T(8,128)(2,1)S(1)}, u32[]{:S(2)}, u32[]{:S(2)}) collective-permute-start(bf16[1152,256]{1,0:T(8,128)(2,1)S(1)} %get-tuple-element.35.refs_1_.refs_2_), channel_id=1, source_target_pairs={{0,1},{1,2},{2,3},{3,4},{4,5},{5,6},{6,7},{7,8},{8,9},{9,10},{10,1... | collective-permute-start | bytes 1769480 | tf_op jit(solution)/shard_map/ppermute | solution.py:353
  65.2 2.1 %collective-permute-start.3 = (bf16[1152,256]{1,0:T(8,128)(2,1)S(1)}, bf16[1152,256]{1,0:T(8,128)(2,1)S(1)}, u32[]{:S(2)}, u32[]{:S(2)}) collective-permute-start(bf16[1152,256]{1,0:T(8,128)(2,1)S(1)} %get-tuple-element.34.refs_0_.refs_1_), channel_id=1, source_target_pairs={{1,0},{2,1},{3,2},{4,3},{5,4},{6,5},{7,6},{8,7},{9,8},{10,9},{11,1... | collective-permute-start | bytes 1769480 | tf_op jit(solution)/shard_map/ppermute | solution.py:354
  67.3 0.1 copy.16.ocean_ref
  67.3 0.0 copy-done.1
  67.4 1.1 ocean_step.2.ocean_ref
  68.5 3.5 %collective-permute-done.2.refs_0_ = bf16[1152,256]{1,0:T(8,128)(2,1)S(1)} collective-permute-done((bf16[1152,256]{1,0:T(8,128)(2,1)S(1)}, bf16[1152,256]{1,0:T(8,128)(2,1)S(1)}, u32[]{:S(2)}, u32[]{:S(2)}) %collective-permute-start.2) | collective-permute-done | bytes 589856 | tf_op jit(solution)/shard_map/ppermute | solution.py:353
  72.0 5.3 %collective-permute-done.3.refs_3_ = bf16[1152,256]{1,0:T(8,128)(2,1)S(1)} collective-permute-done((bf16[1152,256]{1,0:T(8,128)(2,1)S(1)}, bf16[1152,256]{1,0:T(8,128)(2,1)S(1)}, u32[]{:S(2)}, u32[]{:S(2)}) %collective-permute-start.3) | collective-permute-done | bytes 589856 | tf_op jit(solution)/shard_map/ppermute | solution.py:354
  77.3 10.1 %second_step.1.refs_0_ = bf16[1152,512]{1,0:T(8,128)(2,1)} custom-call(bf16[2048,1152]{1,0:T(8,128)(2,1)} %copy-done.3, bf16[1152,2048]{1,0:T(8,128)(2,1)} %copy-done.4, f32[2,1152,128]{2,1,0:T(8,128)S(1)} %broadcast_in_dim.10.drift_ref, f32[2,75,512]{2,1,0:T(8,128)S(1)} %ocean_step.2.ocean_ref, f32[1,512]{1,0:T(1,128)S(1)} %bitcast.25, ...), custom_call_target="tpu_custom_call" | custom-call | flops 4831838208 | bytes 9437184 | tf_op jit(solution)/shard_map/second_step/pallas_call | solution.py:214
  87.4 6.6 %all-to-all-start.2 = ((bf16[16,72,512]{2,1,0:T(8,128)(2,1)}), bf16[16,72,512]{2,1,0:T(8,128)(2,1)S(1)}, u32[]{:S(2)}, u32[]{:S(2)}) async-start(bf16[16,72,512]{2,1,0:T(8,128)(2,1)} %bitcast.5), calls=%async_computation.2 | async-start | bytes 2359296 | tf_op jit(solution)/shard_map/all_to_all | solution.py:307
  94.0 3.4 %collective-permute-start.4 = (f32[2,75,256]{2,1,0:T(8,128)S(1)}, f32[2,75,256]{2,1,0:T(8,128)S(1)}, u32[]{:S(2)}, u32[]{:S(2)}) collective-permute-start(f32[2,75,256]{2,1,0:T(8,128)S(1)} %get-tuple-element.39), channel_id=1, source_target_pairs={{0,1},{1,2},{2,3},{3,4},{4,5},{5,6},{6,7},{7,8},{8,9},{9,10},{10,1... | collective-permute-start | bytes 460808 | tf_op jit(solution)/shard_map/ppermute | solution.py:358
  97.4 1.9 %collective-permute-start.5 = (f32[2,75,256]{2,1,0:T(8,128)S(1)}, f32[2,75,256]{2,1,0:T(8,128)S(1)}, u32[]{:S(2)}, u32[]{:S(2)}) collective-permute-start(f32[2,75,256]{2,1,0:T(8,128)S(1)} %get-tuple-element.38), channel_id=1, source_target_pairs={{1,0},{2,1},{3,2},{4,3},{5,4},{6,5},{7,6},{8,7},{9,8},{10,9},{11,1... | collective-permute-start | bytes 460808 | tf_op jit(solution)/shard_map/ppermute | solution.py:359
  99.3 22.5 %collective-permute-done.4.above_ref = f32[2,75,256]{2,1,0:T(8,128)S(1)} collective-permute-done((f32[2,75,256]{2,1,0:T(8,128)S(1)}, f32[2,75,256]{2,1,0:T(8,128)S(1)}, u32[]{:S(2)}, u32[]{:S(2)}) %collective-permute-start.4) | collective-permute-done | bytes 153632 | tf_op jit(solution)/shard_map/ppermute | solution.py:358
  121.8 1.7 %collective-permute-done.5.below_ref = f32[2,75,256]{2,1,0:T(8,128)S(1)} collective-permute-done((f32[2,75,256]{2,1,0:T(8,128)S(1)}, f32[2,75,256]{2,1,0:T(8,128)S(1)}, u32[]{:S(2)}, u32[]{:S(2)}) %collective-permute-start.5) | collective-permute-done | bytes 153632 | tf_op jit(solution)/shard_map/ppermute | solution.py:359
  123.5 2.4 %ocean_step.3 = f32[2,75,512]{2,1,0:T(8,128)S(1)} custom-call(f32[2,75,512]{2,1,0:T(8,128)S(1)} %ocean_step.2.ocean_ref, f32[2,75,256]{2,1,0:T(8,128)S(1)} %collective-permute-done.4.above_ref, f32[2,75,256]{2,1,0:T(8,128)S(1)} %collective-permute-done.5.below_ref, bf16[2,75,1152]{2,1,0:T(8,128)(2,1)S(1)} %reshape.44.stokes_ref, f32[2,512]{1,0:T(2,128)S(1)} %bitcast.23, ...), custom_call_target="tpu_custom_call" | custom-call | flops 69120000 | bytes 921600 | tf_op jit(solution)/shard_map/ocean_step/pallas_call | solution.py:254
  125.9 0.9 reshape.53
  126.8 0.0 all-to-all-done.2.parts_ref
  126.8 1.6 %gather_rows.1 = bf16[72,32,256]{2,1,0:T(8,128)(2,1)} custom-call(bf16[16,72,512]{2,1,0:T(8,128)(2,1)S(1)} %all-to-all-done.2.parts_ref), custom_call_target="tpu_custom_call" | custom-call | flops 589824 | bytes 2359296 | tf_op jit(solution)/shard_map/gather_rows/pallas_call | solution.py:289
  (9 shorter events, 0.1 us)
Async XLA Ops:
  0.6 13.3 %copy-start.2 = (s32[32,256]{1,0:T(8,128)S(1)}, s32[32,256]{1,0:T(8,128)}, u32[]{:S(2)}) copy-start(s32[32,256]{1,0:T(8,128)} %land_ref.1) | copy-start | bytes 98308
  0.6 13.3 %copy-start = (bf16[72,32,256]{2,1,0:T(8,128)(2,1)S(1)}, bf16[72,32,256]{2,1,0:T(8,128)(2,1)}, u32[]{:S(2)}) copy-start(bf16[72,32,256]{2,1,0:T(8,128)(2,1)} %spec_ref.1) | copy-start | bytes 3538948
  2.1 10.8 %all-to-all-start = ((f32[16,2,2,256]{3,2,1,0:T(2,128)}), f32[16,2,2,256]{3,2,1,0:T(2,128)S(1)}, u32[]{:S(2)}, u32[]{:S(2)}) async-start(f32[16,2,2,256]{3,2,1,0:T(2,128)} %broadcast_in_dim.9), calls=%async_computation | async-start | bytes 131072 | tf_op jit(solution)/shard_map/all_to_all | solution.py:307
  17.9 6.3 %copy-start.5 = (f32[2,75,2,256]{3,2,1,0:T(2,128)S(1)}, f32[2,75,2,256]{3,2,1,0:T(2,128)}, u32[]{:S(2)}) copy-start(f32[2,75,2,256]{3,2,1,0:T(2,128)} %param.10) | copy-start | bytes 921604
  17.9 35.8 %all-to-all-start.1 = ((bf16[16,72,512]{2,1,0:T(8,128)(2,1)}), bf16[16,72,512]{2,1,0:T(8,128)(2,1)S(1)}, u32[]{:S(2)}, u32[]{:S(2)}) async-start(bf16[16,72,512]{2,1,0:T(8,128)(2,1)} %move_bins.1), calls=%async_computation.1 | async-start | bytes 2359296 | tf_op jit(solution)/shard_map/all_to_all | solution.py:307
  25.1 7.8 %copy-start.6 = (f32[2,2,256]{2,1,0:T(2,128)S(1)}, f32[2,2,256]{2,1,0:T(2,128)}, u32[]{:S(2)}) copy-start(f32[2,2,256]{2,1,0:T(2,128)} %param.11) | copy-start | bytes 12292
  25.1 27.0 %collective-permute-start = (f32[2,75,256]{2,1,0:T(8,128)}, f32[2,75,256]{2,1,0:T(8,128)S(1)}, u32[]{:S(2)}, u32[]{:S(2)}) collective-permute-start(f32[2,75,256]{2,1,0:T(8,128)} %bitcast.20), channel_id=1, source_target_pairs={{0,1},{1,2},{2,3},{3,4},{4,5},{5,6},{6,7},{7,8},{8,9},{9,10},{10,1... | collective-permute-start | bytes 460808 | tf_op jit(solution)/shard_map/ppermute | solution.py:332
  29.3 24.3 %collective-permute-start.1 = (f32[2,75,256]{2,1,0:T(8,128)}, f32[2,75,256]{2,1,0:T(8,128)S(1)}, u32[]{:S(2)}, u32[]{:S(2)}) collective-permute-start(f32[2,75,256]{2,1,0:T(8,128)} %bitcast.19), channel_id=1, source_target_pairs={{1,0},{2,1},{3,2},{4,3},{5,4},{6,5},{7,6},{8,7},{9,8},{10,9},{11,1... | collective-permute-start | bytes 460808 | tf_op jit(solution)/shard_map/ppermute | solution.py:333
  47.1 2.1 %copy-start.3 = (bf16[2048,1152]{1,0:T(8,128)(2,1)}, bf16[2048,1152]{1,0:T(8,128)(2,1)S(1)}, u32[]{:S(2)}) copy-start(bf16[2048,1152]{1,0:T(8,128)(2,1)S(1)} %get-tuple-element.24.win_ref) | copy-start | bytes 14155780
  49.2 2.2 %copy-start.4 = (bf16[1152,2048]{1,0:T(8,128)(2,1)}, bf16[1152,2048]{1,0:T(8,128)(2,1)S(1)}, u32[]{:S(2)}) copy-start(bf16[1152,2048]{1,0:T(8,128)(2,1)S(1)} %get-tuple-element.25.wout_ref) | copy-start | bytes 14155780
  53.7 13.7 %copy-start.1 = (f32[75,75]{1,0:T(8,128)S(1)}, f32[75,75]{1,0:T(8,128)}, u32[]{:S(2)}) copy-start(f32[75,75]{1,0:T(8,128)} %inverse_ref.3) | copy-start | bytes 67504
  61.5 10.5 %collective-permute-start.2 = (bf16[1152,256]{1,0:T(8,128)(2,1)S(1)}, bf16[1152,256]{1,0:T(8,128)(2,1)S(1)}, u32[]{:S(2)}, u32[]{:S(2)}) collective-permute-start(bf16[1152,256]{1,0:T(8,128)(2,1)S(1)} %get-tuple-element.35.refs_1_.refs_2_), channel_id=1, source_target_pairs={{0,1},{1,2},{2,3},{3,4},{4,5},{5,6},{6,7},{7,8},{8,9},{9,10},{10,1... | collective-permute-start | bytes 1769480 | tf_op jit(solution)/shard_map/ppermute | solution.py:353
  65.2 12.1 %collective-permute-start.3 = (bf16[1152,256]{1,0:T(8,128)(2,1)S(1)}, bf16[1152,256]{1,0:T(8,128)(2,1)S(1)}, u32[]{:S(2)}, u32[]{:S(2)}) collective-permute-start(bf16[1152,256]{1,0:T(8,128)(2,1)S(1)} %get-tuple-element.34.refs_0_.refs_1_), channel_id=1, source_target_pairs={{1,0},{2,1},{3,2},{4,3},{5,4},{6,5},{7,6},{8,7},{9,8},{10,9},{11,1... | collective-permute-start | bytes 1769480 | tf_op jit(solution)/shard_map/ppermute | solution.py:354
  87.4 39.4 %all-to-all-start.2 = ((bf16[16,72,512]{2,1,0:T(8,128)(2,1)}), bf16[16,72,512]{2,1,0:T(8,128)(2,1)S(1)}, u32[]{:S(2)}, u32[]{:S(2)}) async-start(bf16[16,72,512]{2,1,0:T(8,128)(2,1)} %bitcast.5), calls=%async_computation.2 | async-start | bytes 2359296 | tf_op jit(solution)/shard_map/all_to_all | solution.py:307
  94.0 27.8 %collective-permute-start.4 = (f32[2,75,256]{2,1,0:T(8,128)S(1)}, f32[2,75,256]{2,1,0:T(8,128)S(1)}, u32[]{:S(2)}, u32[]{:S(2)}) collective-permute-start(f32[2,75,256]{2,1,0:T(8,128)S(1)} %get-tuple-element.39), channel_id=1, source_target_pairs={{0,1},{1,2},{2,3},{3,4},{4,5},{5,6},{6,7},{7,8},{8,9},{9,10},{10,1... | collective-permute-start | bytes 460808 | tf_op jit(solution)/shard_map/ppermute | solution.py:358
  97.4 26.1 %collective-permute-start.5 = (f32[2,75,256]{2,1,0:T(8,128)S(1)}, f32[2,75,256]{2,1,0:T(8,128)S(1)}, u32[]{:S(2)}, u32[]{:S(2)}) collective-permute-start(f32[2,75,256]{2,1,0:T(8,128)S(1)} %get-tuple-element.38), channel_id=1, source_target_pairs={{1,0},{2,1},{3,2},{4,3},{5,4},{6,5},{7,6},{8,7},{9,8},{10,9},{11,1... | collective-permute-start | bytes 460808 | tf_op jit(solution)/shard_map/ppermute | solution.py:359
